TPU v7x, 32 devices: a whole 2x2x4 slice. The times are simulated.
32 devices in a mesh: dp: 32 (over z, y, x, core).
Axes of the slice: x: 2, y: 2, z: 4, core: 2. Of those that a mesh axis runs over, the one named last changes fastest.
Arguments:
- patches: bfloat16 [24576, 1280], P('dp'), may hold values from -6 to 6
- patch_grids: int32 [192, 4, 2], P('dp'), may hold values from 0 to 16, as said below
- block_counts: int32 [32], replicated, may hold values from 0 to 6, as said below
- send_counts: int32 [5, 32], replicated, may hold values from 0 to 2, as said below
- row_table: bfloat16 [16, 1280], replicated, may hold values from -3 to 3
- col_table: bfloat16 [16, 1280], replicated, may hold values from -3 to 3
- ln_gain: bfloat16 [1280], replicated, may hold values from 0.25 to 1.75
- ln_bias: bfloat16 [1280], replicated, may hold values from -3 to 3
- w_qkv: bfloat16 [1280, 1920], replicated, may hold values from -1.2 to 1.2
- b_qkv: bfloat16 [1920], replicated, may hold values from -3 to 3
- w_out: bfloat16 [640, 1280], replicated, may hold values from -0.25 to 0.25
- b_out: bfloat16 [1280], replicated, may hold values from -3 to 3
- cotangent: bfloat16 [16384, 1280], P('dp'), may hold values from -3 to 3
Outputs:
- block_output: bfloat16 [16384, 1280], P('dp')
- grad_w_qkv: float32 [1280, 1920], P('dp')
- grad_w_out: float32 [640, 1280], P('dp')
Inputs may be any that keep to these rules, and one draw needn't show every extreme that they name: `patch_grids`: in each block slot the areas h * w of its 4 images sum to at most 128; heights are 1 to 16, widths 0 to 16, width 0 meaning no image. `block_counts`: live blocks of each rank at the start; with send_counts no rank holds more than 6 live blocks during balancing, and after the last section every rank holds 2 to 4, some rank exactly 4. `send_counts`: A rank never sends more blocks than it holds live; of two partners in a section at most one sends; in every draw some rank sends exactly 2 blocks in the last section.
All inputs are finite; a program needn't handle non-finite values.
Results may differ from a plain program's by a relative error of at most 0.0075.
Values may be sent and summed in bfloat16 or wider, within the bound.
A program may use at most 128 MiB of HBM per device.

v0:
```python
import math

import jax
import jax.numpy as jnp
from jax import lax
from jax.sharding import PartitionSpec as P

HEAD = 80
BLOCK = 128


EPSILON = 1e-06


def partner_2(value, axis, stride):
    return lax.ppermute(value, axis, [(i, i ^ 1 << stride) for i in range(lax.axis_size(axis))])


def token_layout(patch_grids):
    heights = patch_grids[:, :, 0]
    widths = patch_grids[:, :, 1]
    image_area = heights * widths
    image_end = jnp.cumsum(image_area, axis=1)
    image_start = image_end - image_area
    positions = jnp.arange(BLOCK, dtype=jnp.int32)[None, :, None]
    member = ((positions >= image_start[:, None, :]) & (positions < image_end[:, None, :])).astype(
        jnp.int32
    )
    image_ids = jnp.arange(patch_grids.shape[1], dtype=jnp.int32)
    in_image = jnp.sum(member, axis=-1)
    segment = jnp.sum(member * image_ids, axis=-1) + in_image - 1
    offset = positions[:, :, 0] - jnp.sum(member * image_start[:, None, :], axis=-1)
    offset = offset * in_image
    span = jnp.maximum(jnp.sum(member * widths[:, None, :], axis=-1), 1)
    row_index = offset // span
    col_index = offset - row_index * span
    return (segment, row_index, col_index, in_image)


def embed_blocks(patch_rows, patch_grids, row_table, col_table):
    block_total = patch_grids.shape[0]
    segment, row_index, col_index, in_image = token_layout(patch_grids)
    levels = jnp.arange(row_table.shape[0], dtype=jnp.int32)
    row_hot = (row_index.reshape(-1, 1) == levels[None, :]).astype(jnp.bfloat16)
    col_hot = (col_index.reshape(-1, 1) == levels[None, :]).astype(jnp.bfloat16)
    table_sum = jnp.dot(row_hot, row_table, preferred_element_type=jnp.float32) + jnp.dot(
        col_hot, col_table, preferred_element_type=jnp.float32
    )
    embedded = (
        patch_rows.astype(jnp.float32) + table_sum * in_image.reshape(-1, 1).astype(jnp.float32)
    ).astype(jnp.bfloat16)
    return (embedded.reshape(block_total, BLOCK, patch_rows.shape[1]), segment)


def layer_forward(blocks, marks, ln_gain, ln_bias, w_qkv, b_qkv, w_out, b_out):
    block_total = blocks.shape[0]
    model_width = blocks.shape[2]
    inner = w_out.shape[0]
    head_count = inner // HEAD
    rows = blocks.reshape(block_total * BLOCK, model_width).astype(jnp.float32)
    average = jnp.mean(rows, axis=-1, keepdims=True)
    centred = rows - average
    variance = jnp.mean(centred * centred, axis=-1, keepdims=True)
    normed = (
        centred * lax.rsqrt(variance + EPSILON) * ln_gain.astype(jnp.float32)
        + ln_bias.astype(jnp.float32)
    ).astype(jnp.bfloat16)
    mixed = (
        jnp.dot(normed, w_qkv, preferred_element_type=jnp.float32) + b_qkv.astype(jnp.float32)
    ).astype(jnp.bfloat16)
    shaped = mixed.reshape(block_total, BLOCK, 3, head_count, HEAD).astype(jnp.float32)
    query_f = shaped[:, :, 0]
    key_f = shaped[:, :, 1]
    value_f = shaped[:, :, 2]
    score_scale = 1.0 / math.sqrt(HEAD)
    scores = jnp.einsum("bqhd,bkhd->bhqk", query_f, key_f) * score_scale
    same_image = marks[:, :, None] == marks[:, None, :]
    scores = jnp.where(same_image[:, None], scores, -1e30)
    top_score = jnp.max(scores, axis=-1, keepdims=True)
    expo = jnp.exp(scores - top_score)
    probs_f = expo / jnp.sum(expo, axis=-1, keepdims=True)
    probs_b = probs_f.astype(jnp.bfloat16)
    attended = jnp.einsum("bhqk,bkhd->bqhd", probs_b.astype(jnp.float32), value_f)
    attended = attended.reshape(block_total * BLOCK, inner).astype(jnp.bfloat16)
    projected = jnp.dot(attended, w_out, preferred_element_type=jnp.float32) + b_out.astype(
        jnp.float32
    )
    result = (rows + projected).astype(jnp.bfloat16)
    return (result, (normed, query_f, key_f, value_f, probs_f, probs_b, attended))


def output_backward(out_grad, saved, w_out):
    normed, query_f, key_f, value_f, probs_f, probs_b, attended = saved
    grad_out = jnp.dot(attended.T, out_grad, preferred_element_type=jnp.float32)
    attn_grad = jnp.dot(out_grad, w_out.T, preferred_element_type=jnp.float32)
    return (grad_out, attn_grad.reshape(query_f.shape))


def qkv_backward(attn_grad, saved):
    normed, query_f, key_f, value_f, probs_f, probs_b, attended = saved
    score_scale = 1.0 / math.sqrt(HEAD)
    prob_grad = jnp.einsum("bqhd,bkhd->bhqk", attn_grad, value_f)
    value_grad = jnp.einsum("bhqk,bqhd->bkhd", probs_b.astype(jnp.float32), attn_grad)
    score_grad = (
        probs_f * (prob_grad - jnp.sum(prob_grad * probs_f, axis=-1, keepdims=True)) * score_scale
    )
    query_grad = jnp.einsum("bhqk,bkhd->bqhd", score_grad, key_f)
    key_grad = jnp.einsum("bhqk,bqhd->bkhd", score_grad, query_f)
    row_total = query_f.shape[0] * query_f.shape[1]
    mixed_grad = (
        jnp.stack([query_grad, key_grad, value_grad], axis=2)
        .reshape(row_total, -1)
        .astype(jnp.bfloat16)
    )
    return jnp.dot(normed.T, mixed_grad, preferred_element_type=jnp.float32)


def local(
    patches,
    patch_grids,
    block_counts,
    send_counts,
    row_table,
    col_table,
    ln_gain,
    ln_bias,
    w_qkv,
    b_qkv,
    w_out,
    b_out,
    cotangent,
):
    slot_count = patches.shape[0] // BLOCK
    balanced = cotangent.shape[0] // BLOCK
    spare_slots = slot_count - balanced
    embedded, segment = embed_blocks(patches, patch_grids, row_table, col_table)
    segment_marks = segment.astype(jnp.bfloat16)
    all_ranks = jnp.arange(block_counts.shape[0], dtype=jnp.int32)
    own_rank = lax.axis_index("dp")
    counts = block_counts
    slot_ids = jnp.arange(slot_count, dtype=jnp.int32)
    section_total = lax.axis_size("dp").bit_length() - 1
    for section_index in range(section_total):
        partner = jnp.bitwise_xor(all_ranks, 1 << section_index)
        sent_now = send_counts[section_index]
        received = sent_now[partner]
        own_count = counts[own_rank]
        leaving = sent_now[own_rank]
        arriving = received[own_rank]
        staying = slot_ids < own_count - leaving
        landing = (slot_ids >= own_count) & (slot_ids < own_count + arriving)
        picked = jnp.clip(
            own_count - leaving + jnp.arange(spare_slots, dtype=jnp.int32), 0, slot_count - 1
        )
        far_blocks, far_marks = partner_2(
            (jnp.take(embedded, picked, axis=0), jnp.take(segment_marks, picked, axis=0)),
            "dp",
            section_index,
        )
        source = jnp.clip(slot_ids - own_count, 0, spare_slots - 1)
        arrived = jnp.take(far_blocks, source, axis=0)
        arrived_marks = jnp.take(far_marks, source, axis=0)
        embedded = jnp.where(
            staying[:, None, None],
            embedded,
            jnp.where(landing[:, None, None], arrived, jnp.zeros_like(embedded)),
        )
        segment_marks = jnp.where(
            staying[:, None],
            segment_marks,
            jnp.where(landing[:, None], arrived_marks, -jnp.ones_like(segment_marks)),
        )
        counts = counts - sent_now + received
    live_count = counts[own_rank]
    rank_blocks = embedded[:balanced]
    rank_marks = segment_marks[:balanced]
    rank_live = jnp.arange(balanced, dtype=jnp.int32) < live_count
    result, saved = layer_forward(
        rank_blocks, rank_marks, ln_gain, ln_bias, w_qkv, b_qkv, w_out, b_out
    )
    slot_live = jnp.repeat(rank_live, BLOCK).reshape(-1, 1)
    result = jnp.where(slot_live, result, jnp.zeros_like(result))
    token_live = (rank_live[:, None] & (rank_marks >= 0)).reshape(-1, 1)
    out_grad = jnp.where(token_live, cotangent, jnp.zeros_like(cotangent))
    grad_out, attn_grad = output_backward(out_grad, saved, w_out)
    grad_qkv = qkv_backward(attn_grad, saved)
    qkv_rows, out_rows = (
        lax.psum_scatter(grad_qkv, "dp", scatter_dimension=0, tiled=True),
        lax.psum_scatter(grad_out, "dp", scatter_dimension=0, tiled=True),
    )
    return (result, qkv_rows, out_rows)


def solution(mesh):
    return jax.shard_map(
        local,
        mesh=mesh,
        in_specs=(
            P("dp", None),
            P("dp", None, None),
            P(),
            P(),
            P(),
            P(),
            P(),
            P(),
            P(),
            P(),
            P(),
            P(),
            P("dp", None),
        ),
        out_specs=(P("dp", None), P("dp", None), P("dp", None)),
        check_vma=False,
    )
```

profile of v0, /device:TPU:0, one launch (start us, length us, event | category | flops | bytes accessed | tf_op | source)
XLA Modules:
  0.0 367.3 jit_solution(13566548193083122917)
XLA Ops:
  15.5 2.2 fusion.5
  52.6 3.7 %fusion.18 = bf16[6,128,1280]{2,1,0:T(8,128)(2,1)} fusion(bf16[6,128,1280]{2,1,0:T(8,128)(2,1)} %bitcast.183, bf16[6,128,1280]{2,1,0:T(8,128)(2,1)} %gather_fusion.6, pred[6]{0:T(512)(128)(4,1)S(1)} %get-tuple-element.51, pred[6]{0:T(512)(128)(4,1)S(1)} %get-tuple-element.52, pred[6]{0:T(512)(128)(4,1)S(1)} %iota_compare_fusion.6), kind=kLoop, calls=%fused_computation.58 | loop fusion | flops 2949120 | bytes 5898258 | tf_op jit(solution)/shard_map/jit(_where)/select_n | solution.py:163
  56.4 2.1 gather_fusion.7
  58.6 3.0 collective-permute-start.1
  61.8 14.9 %collective-permute-done.6 = bf16[2,128]{1,0:T(2,128)(2,1)S(1)} collective-permute-done((bf16[2,128]{1,0:T(2,128)(2,1)S(1)}, bf16[2,128]{1,0:T(2,128)(2,1)S(1)}, u32[]{:S(2)}, u32[]{:S(2)}) %collective-permute-start.6) | collective-permute-done | bytes 544 | tf_op jit(solution)/shard_map/ppermute | solution.py:16
  81.8 3.7 %fusion.17 = bf16[6,128,1280]{2,1,0:T(8,128)(2,1)} fusion(bf16[6,128,1280]{2,1,0:T(8,128)(2,1)} %fusion.18, bf16[6,128,1280]{2,1,0:T(8,128)(2,1)} %gather_fusion.8, pred[6]{0:T(512)(128)(4,1)S(1)} %get-tuple-element.53, pred[6]{0:T(512)(128)(4,1)S(1)} %get-tuple-element.54, pred[6]{0:T(512)(128)(4,1)S(1)} %iota_compare_fusion.7), kind=kLoop, calls=%fused_computation.56 | loop fusion | flops 2949120 | bytes 5898258 | tf_op jit(solution)/shard_map/jit(_where)/select_n | solution.py:163
  93.5 9.8 %collective-permute-done.2 = bf16[2,128,1280]{2,1,0:T(8,128)(2,1)S(1)} collective-permute-done((bf16[2,128,1280]{2,1,0:T(8,128)(2,1)S(1)}, bf16[2,128,1280]{2,1,0:T(8,128)(2,1)S(1)}, u32[]{:S(2)}, u32[]{:S(2)}) %collective-permute-start.2) | collective-permute-done | bytes 655392 | tf_op jit(solution)/shard_map/ppermute | solution.py:16
  105.3 3.7 %fusion.16 = bf16[6,128,1280]{2,1,0:T(8,128)(2,1)} fusion(bf16[6,128,1280]{2,1,0:T(8,128)(2,1)} %fusion.17, bf16[6,128,1280]{2,1,0:T(8,128)(2,1)} %gather_fusion.10, pred[6]{0:T(512)(128)(4,1)S(1)} %get-tuple-element.55, pred[6]{0:T(512)(128)(4,1)S(1)} %get-tuple-element.56, pred[6]{0:T(512)(128)(4,1)S(1)} %iota_compare_fusion.8), kind=kLoop, calls=%fused_computation.54 | loop fusion | flops 2949120 | bytes 5898258 | tf_op jit(solution)/shard_map/jit(_where)/select_n | solution.py:163
  109.0 2.2 gather_fusion.11
  113.7 2.6 collective-permute-start.9
  117.0 8.1 %collective-permute-done.9 = bf16[2,128]{1,0:T(2,128)(2,1)S(1)} collective-permute-done((bf16[2,128]{1,0:T(2,128)(2,1)S(1)}, bf16[2,128]{1,0:T(2,128)(2,1)S(1)}, u32[]{:S(2)}, u32[]{:S(2)}) %collective-permute-start.9) | collective-permute-done | bytes 544 | tf_op jit(solution)/shard_map/ppermute | solution.py:16
  128.0 3.7 %fusion.15 = bf16[6,128,1280]{2,1,0:T(8,128)(2,1)} fusion(bf16[6,128,1280]{2,1,0:T(8,128)(2,1)} %fusion.16, bf16[6,128,1280]{2,1,0:T(8,128)(2,1)} %gather_fusion.12, pred[6]{0:T(512)(128)(4,1)S(1)} %get-tuple-element.57, pred[6]{0:T(512)(128)(4,1)S(1)} %get-tuple-element.58, pred[6]{0:T(512)(128)(4,1)S(1)} %iota_compare_fusion.9), kind=kLoop, calls=%fused_computation.52 | loop fusion | flops 2949120 | bytes 5898258 | tf_op jit(solution)/shard_map/jit(_where)/select_n | solution.py:163
  134.0 3.2 collective-permute-start.4
  137.3 3.3 fusion.43
  140.6 2.3 reshape.393
  143.1 19.9 %collective-permute-done.4 = bf16[2,128,1280]{2,1,0:T(8,128)(2,1)S(1)} collective-permute-done((bf16[2,128,1280]{2,1,0:T(8,128)(2,1)S(1)}, bf16[2,128,1280]{2,1,0:T(8,128)(2,1)S(1)}, u32[]{:S(2)}, u32[]{:S(2)}) %collective-permute-start.4) | collective-permute-done | bytes 655392 | tf_op jit(solution)/shard_map/ppermute | solution.py:16
  165.0 2.4 convert_reduce_fusion
  168.5 6.5 %add_convert_fusion = bf16[512,1920]{1,0:T(8,128)(2,1)} fusion(bf16[512,1280]{1,0:T(8,128)(2,1)S(1)} %fusion.11, bf16[1280,1920]{1,0:T(8,128)(2,1)} %param.29, f32[1920]{0:T(1024)S(1)} %convert_element_type.98), kind=kOutput, calls=%fused_computation.29 | convolution fusion | flops 2518548480 | bytes 8199680 | tf_op jit(solution)/shard_map/dot_general | solution.py:69
  174.9 6.4 %reshape.655 = bf16[4,128,3,8,80]{4,3,2,1,0:T(8,128)(2,1)} reshape(bf16[512,1920]{1,0:T(8,128)(2,1)} %add_convert_fusion) | data formatting | bytes 3932160 | tf_op jit(solution)/shard_map/reshape | solution.py:71
  181.3 3.6 fusion.84
  184.9 2.3 copy.84
  187.3 2.3 copy.83
  189.6 2.3 copy.85
  191.9 3.5 fusion.87
  195.4 2.8 fusion.24
  203.2 5.6 %fusion.12 = f32[1280,1920]{1,0:T(8,128)} fusion(bf16[512,1280]{1,0:T(8,128)(2,1)S(1)} %bitcast.187, bf16[240,8,4,128]{3,2,1,0:T(4,128)(2,1)S(1)} %bitcast.186), kind=kOutput, calls=%fused_computation.47 | convolution fusion | flops 2516582400 | bytes 13107200 | tf_op jit(solution)/shard_map/dot_general | solution.py:115
  208.9 2.4 fusion.21
  212.6 2.9 fusion.31
  215.6 92.3 %fusion = f32[24,1280]{1,0:T(8,128)S(1)} fusion(f32[640,1280]{1,0:T(8,128)} %fusion.31), kind=kCustom, calls=%all-reduce-scatter | all-reduce-scatter fusion | flops 983041 | bytes 3399680
  316.4 3.5 fusion.7
  320.6 2.7 concatenate
  323.9 36.5 %reduce-scatter.6.cloned.1.call-done = f32[40,1920]{1,0:T(8,128)} async-done(((f32[1280,1920]{1,0:T(8,128)}), f32[40,1920]{1,0:T(8,128)}) %reduce-scatter.6.cloned.1.call-update) | async-done | bytes 307216
  (195 shorter events, 73.4 us)
Async XLA Ops:
  7.2 130.1 %copy-start = (bf16[640,1280]{1,0:T(8,128)(2,1)S(1)}, bf16[640,1280]{1,0:T(8,128)(2,1)}, u32[]{:S(2)}) copy-start(bf16[640,1280]{1,0:T(8,128)(2,1)} %param.31) | copy-start | bytes 4915204
  7.2 353.3 %reduce-scatter.6.cloned.1.call-start = ((), (), s32[]{:S(2)}) async-start(), calls=%async_computation.1 | async-start | bytes 10137600
  13.2 36.3 %collective-permute-start.5 = (bf16[2,128]{1,0:T(2,128)(2,1)S(1)}, bf16[2,128]{1,0:T(2,128)(2,1)S(1)}, u32[]{:S(2)}, u32[]{:S(2)}) collective-permute-start(bf16[2,128]{1,0:T(2,128)(2,1)S(1)} %broadcast_select_fusion.12), channel_id=1, source_target_pairs={{0,1},{1,0},{2,3},{3,2},{4,5},{5,4},{6,7},{7,6},{8,9},{9,8},{10,11... | collective-permute-start | bytes 1544 | tf_op jit(solution)/shard_map/ppermute | solution.py:16
  13.8 1.7 copy-start.2
  13.8 1.7 copy-start.9
  19.8 7.6 %copy-start.11 = (s32[5,32]{1,0:T(8,128)S(1)}, s32[5,32]{1,0:T(8,128)}, u32[]{:S(2)}) copy-start(s32[5,32]{1,0:T(8,128)} %param.24) | copy-start | bytes 1924
  19.9 7.6 %copy-start.16 = (s32[32]{0:T(128)S(1)}, s32[32]{0:T(128)}, u32[]{:S(2)}) copy-start(s32[32]{0:T(128)} %param.23) | copy-start | bytes 388
  20.0 30.6 %collective-permute-start = (bf16[2,128,1280]{2,1,0:T(8,128)(2,1)S(1)}, bf16[2,128,1280]{2,1,0:T(8,128)(2,1)S(1)}, u32[]{:S(2)}, u32[]{:S(2)}) collective-permute-start(bf16[2,128,1280]{2,1,0:T(8,128)(2,1)S(1)} %broadcast_select_fusion.5), channel_id=1, source_target_pairs={{0,1},{1,0},{2,3},{3,2},{4,5},{5,4},{6,7},{7,6},{8,9},{9,8},{10,11... | collective-permute-start | bytes 1966088 | tf_op jit(solution)/shard_map/ppermute | solution.py:16
  58.6 21.1 %collective-permute-start.1 = (bf16[2,128,1280]{2,1,0:T(8,128)(2,1)S(1)}, bf16[2,128,1280]{2,1,0:T(8,128)(2,1)S(1)}, u32[]{:S(2)}, u32[]{:S(2)}) collective-permute-start(bf16[2,128,1280]{2,1,0:T(8,128)(2,1)S(1)} %broadcast_select_fusion.4), channel_id=1, source_target_pairs={{0,2},{1,3},{2,0},{3,1},{4,6},{5,7},{6,4},{7,5},{8,10},{9,11},{10,... | collective-permute-start | bytes 1966088 | tf_op jit(solution)/shard_map/ppermute | solution.py:16
  61.7 14.9 %collective-permute-start.6 = (bf16[2,128]{1,0:T(2,128)(2,1)S(1)}, bf16[2,128]{1,0:T(2,128)(2,1)S(1)}, u32[]{:S(2)}, u32[]{:S(2)}) collective-permute-start(bf16[2,128]{1,0:T(2,128)(2,1)S(1)} %broadcast_select_fusion.11), channel_id=1, source_target_pairs={{0,2},{1,3},{2,0},{3,1},{4,6},{5,7},{6,4},{7,5},{8,10},{9,11},{10,... | collective-permute-start | bytes 1544 | tf_op jit(solution)/shard_map/ppermute | solution.py:16
  78.0 10.1 %collective-permute-start.7 = (bf16[2,128]{1,0:T(2,128)(2,1)S(1)}, bf16[2,128]{1,0:T(2,128)(2,1)S(1)}, u32[]{:S(2)}, u32[]{:S(2)}) collective-permute-start(bf16[2,128]{1,0:T(2,128)(2,1)S(1)} %broadcast_select_fusion.10), channel_id=1, source_target_pairs={{0,4},{1,5},{2,6},{3,7},{4,0},{5,1},{6,2},{7,3},{8,12},{9,13},{10,... | collective-permute-start | bytes 1544 | tf_op jit(solution)/shard_map/ppermute | solution.py:16
  87.8 15.5 %collective-permute-start.2 = (bf16[2,128,1280]{2,1,0:T(8,128)(2,1)S(1)}, bf16[2,128,1280]{2,1,0:T(8,128)(2,1)S(1)}, u32[]{:S(2)}, u32[]{:S(2)}) collective-permute-start(bf16[2,128,1280]{2,1,0:T(8,128)(2,1)S(1)} %broadcast_select_fusion.3), channel_id=1, source_target_pairs={{0,4},{1,5},{2,6},{3,7},{4,0},{5,1},{6,2},{7,3},{8,12},{9,13},{10,... | collective-permute-start | bytes 1966088 | tf_op jit(solution)/shard_map/ppermute | solution.py:16
  89.4 3.6 collective-permute-start.8
  109.0 7.9 %copy-start.12 = (bf16[1280]{0:T(1024)(128)(2,1)S(1)}, bf16[1280]{0:T(1024)(128)(2,1)}, u32[]{:S(2)}) copy-start(bf16[1280]{0:T(1024)(128)(2,1)} %param.27) | copy-start | bytes 7684
  109.0 7.9 %copy-start.13 = (bf16[1280]{0:T(1024)(128)(2,1)S(1)}, bf16[1280]{0:T(1024)(128)(2,1)}, u32[]{:S(2)}) copy-start(bf16[1280]{0:T(1024)(128)(2,1)} %param.28) | copy-start | bytes 7684
  109.0 8.0 %copy-start.14 = (bf16[1920]{0:T(1024)(128)(2,1)S(1)}, bf16[1920]{0:T(1024)(128)(2,1)}, u32[]{:S(2)}) copy-start(bf16[1920]{0:T(1024)(128)(2,1)} %param.30) | copy-start | bytes 11524
  111.3 14.7 %collective-permute-start.3 = (bf16[2,128,1280]{2,1,0:T(8,128)(2,1)S(1)}, bf16[2,128,1280]{2,1,0:T(8,128)(2,1)S(1)}, u32[]{:S(2)}, u32[]{:S(2)}) collective-permute-start(bf16[2,128,1280]{2,1,0:T(8,128)(2,1)S(1)} %broadcast_select_fusion.2), channel_id=1, source_target_pairs={{0,8},{1,9},{2,10},{3,11},{4,12},{5,13},{6,14},{7,15},{8,0},{9,1},... | collective-permute-start | bytes 1966088 | tf_op jit(solution)/shard_map/ppermute | solution.py:16
  113.7 11.4 %collective-permute-start.9 = (bf16[2,128]{1,0:T(2,128)(2,1)S(1)}, bf16[2,128]{1,0:T(2,128)(2,1)S(1)}, u32[]{:S(2)}, u32[]{:S(2)}) collective-permute-start(bf16[2,128]{1,0:T(2,128)(2,1)S(1)} %broadcast_select_fusion.8), channel_id=1, source_target_pairs={{0,16},{1,17},{2,18},{3,19},{4,20},{5,21},{6,22},{7,23},{8,24},{9,... | collective-permute-start | bytes 1544 | tf_op jit(solution)/shard_map/ppermute | solution.py:16
  125.8 11.5 %copy-start.10 = (bf16[6,128]{1,0:T(8,128)(2,1)}, bf16[6,128]{1,0:T(8,128)(2,1)S(1)}, u32[]{:S(2)}) copy-start(bf16[6,128]{1,0:T(8,128)(2,1)S(1)} %fusion.62) | copy-start | bytes 4612
  134.0 28.9 %collective-permute-start.4 = (bf16[2,128,1280]{2,1,0:T(8,128)(2,1)S(1)}, bf16[2,128,1280]{2,1,0:T(8,128)(2,1)S(1)}, u32[]{:S(2)}, u32[]{:S(2)}) collective-permute-start(bf16[2,128,1280]{2,1,0:T(8,128)(2,1)S(1)} %broadcast_select_fusion.1), channel_id=1, source_target_pairs={{0,16},{1,17},{2,18},{3,19},{4,20},{5,21},{6,22},{7,23},{8,24},{9,... | collective-permute-start | bytes 1966088 | tf_op jit(solution)/shard_map/ppermute | solution.py:16
  137.3 5.6 %slice-start = ((bf16[6,128]{1,0:T(8,128)(2,1)}), bf16[4,128]{1,0:T(4,128)(2,1)S(1)}, s32[]{:S(2)}) async-start(bf16[6,128]{1,0:T(8,128)(2,1)} %copy-done.10), calls=%async_computation.2 | async-start | bytes 2048 | tf_op jit(solution)/shard_map/slice | solution.py:176
  195.4 2.8 copy-start.4
  195.4 2.8 copy-start.5
  195.4 2.8 copy-start.17
  208.9 3.8 %copy-start.3 = (bf16[512,1280]{1,0:T(8,128)(2,1)S(1)}, bf16[512,1280]{1,0:T(8,128)(2,1)}, u32[]{:S(2)}) copy-start(bf16[512,1280]{1,0:T(8,128)(2,1)} %param.33) | copy-start | bytes 3932164
  215.6 93.6 %copy-start.15 = (bf16[1280]{0:T(1024)(128)(2,1)S(1)}, bf16[1280]{0:T(1024)(128)(2,1)}, u32[]{:S(2)}) copy-start(bf16[1280]{0:T(1024)(128)(2,1)} %param.32) | copy-start | bytes 7684
  307.9 6.5 %collective-permute-start.15 = (f32[4,1280]{1,0:T(4,128)S(1)}, f32[4,1280]{1,0:T(4,128)S(1)}, u32[]{:S(2)}, u32[]{:S(2)}) collective-permute-start(f32[4,1280]{1,0:T(4,128)S(1)} %slice.106), channel_id=1, source_target_pairs={{0,6},{1,7},{2,8},{3,9},{4,10},{5,11},{6,12},{7,13},{8,14},{9,15},... | collective-permute-start | bytes 61448
  309.2 10.7 %collective-permute-start.14 = (f32[24,1280]{1,0:T(8,128)S(1)}, f32[24,1280]{1,0:T(8,128)S(1)}, u32[]{:S(2)}, u32[]{:S(2)}) collective-permute-start(f32[24,1280]{1,0:T(8,128)S(1)} %fusion), channel_id=1, source_target_pairs={{0,5},{1,6},{2,7},{3,8},{4,9},{5,10},{6,11},{7,12},{8,13},{9,14},{... | collective-permute-start | bytes 368648
  310.5 9.4 %collective-permute-start.13 = (f32[24,1280]{1,0:T(8,128)S(1)}, f32[24,1280]{1,0:T(8,128)S(1)}, u32[]{:S(2)}, u32[]{:S(2)}) collective-permute-start(f32[24,1280]{1,0:T(8,128)S(1)} %fusion), channel_id=1, source_target_pairs={{0,4},{1,5},{2,6},{3,7},{4,8},{5,9},{6,10},{7,11},{8,12},{9,13},{1... | collective-permute-start | bytes 368648
  311.8 8.1 %collective-permute-start.12 = (f32[24,1280]{1,0:T(8,128)S(1)}, f32[24,1280]{1,0:T(8,128)S(1)}, u32[]{:S(2)}, u32[]{:S(2)}) collective-permute-start(f32[24,1280]{1,0:T(8,128)S(1)} %fusion), channel_id=1, source_target_pairs={{0,3},{1,4},{2,5},{3,6},{4,7},{5,8},{6,9},{7,10},{8,11},{9,12},{10... | collective-permute-start | bytes 368648
  313.1 6.8 %collective-permute-start.11 = (f32[24,1280]{1,0:T(8,128)S(1)}, f32[24,1280]{1,0:T(8,128)S(1)}, u32[]{:S(2)}, u32[]{:S(2)}) collective-permute-start(f32[24,1280]{1,0:T(8,128)S(1)} %fusion), channel_id=1, source_target_pairs={{0,2},{1,3},{2,4},{3,5},{4,6},{5,7},{6,8},{7,9},{8,10},{9,11},{10,... | collective-permute-start | bytes 368648
  314.5 6.1 %collective-permute-start.10 = (f32[24,1280]{1,0:T(8,128)S(1)}, f32[24,1280]{1,0:T(8,128)}, u32[]{:S(2)}, u32[]{:S(2)}) collective-permute-start(f32[24,1280]{1,0:T(8,128)S(1)} %fusion), channel_id=1, source_target_pairs={{0,1},{1,2},{2,3},{3,4},{4,5},{5,6},{6,7},{7,8},{8,9},{9,10},{10,1... | collective-permute-start | bytes 368648
  (4 other events, 3.6 us)
Sparse Core Ops, SparseCore 0:
  209.0 151.3 reduce-scatter.5
where the time goes:
time: 369 us; the launch traced here: 367 us
  blocking collectives  92.3 us (25%)
  waiting for transfers between devices  90.6 us (25%)
  local copies, waits for them, and re-layouts  69.2 us (19%)
  matrix products  36.3 us (10%)
  other arithmetic  28.2 us (8%)
  between operations  27.3 us (7%)
  starting transfers between devices  23.4 us (6%)
    unnamed x1, blocking collectives  92.3 us
    ppermute x10, waiting for transfers between devices, partner_2(): lax.ppermute(value, axis, [(i, i ^ 1 << stride) for i in range(lax.axis_s...  54 us
    unnamed x8, waiting for transfers between devices  36.5 us
    ppermute x10, starting transfers between devices, partner_2(): lax.ppermute(value, axis, [(i, i ^ 1 << stride) for i in range(lax.axis_s...  15 us
    select_n x4, other arithmetic, local(): jnp.where(staying[:, None, None], embedded, jnp.where(landing[:, None, No...  14.9 us
    unnamed x42, local copies, waits for them, and re-layouts  12.6 us
    gather x5, local copies, waits for them, and re-layouts, local(): jnp.take(embedded, picked, axis=0)  10.7 us
    gather x5, local copies, waits for them, and re-layouts, local(): arrived = jnp.take(far_blocks, source, axis=0)  10.1 us
  transfers between devices with their start and end apart: 17, of which 7 were waited for; matrix products, arithmetic and copies ran while one was open for 41% of the time, Pallas kernels for 0%

commit v1 on v0

--- a/solution.py
+++ b/solution.py
@@ -1,19 +1,273 @@
+import functools
 import math
 
 import jax
 import jax.numpy as jnp
 from jax import lax
+from jax.experimental import pallas as pl
+from jax.experimental.pallas import tpu as pltpu
 from jax.sharding import PartitionSpec as P
 
 HEAD = 80
 BLOCK = 128
-
-
+CHUNKS = 8
 EPSILON = 1e-06
-
-
-def partner_2(value, axis, stride):
-    return lax.ppermute(value, axis, [(i, i ^ 1 << stride) for i in range(lax.axis_size(axis))])
+MESH = pl.DeviceIdType.MESH
+
+
+def partner_of(me, bit):
+    own = (me // (1 << bit)) % 2
+    return me + (1 - 2 * own) * (1 << bit)
+
+
+def greet_partners(me, bits):
+    barrier = pltpu.get_barrier_semaphore()
+    for bit in range(bits):
+        pl.semaphore_signal(
+            barrier, inc=1, device_id=(partner_of(me, bit),), device_id_type=MESH
+        )
+    pl.semaphore_wait(barrier, bits)
+
+
+def balance_kernel(
+    sections, counts_ref, sends_ref, patches_ref, marks_ref, rows_ref, tags_ref,
+    slots, slot_tags, stage, stage_tags, land, land_tags, sent, landed, sent_tags, landed_tags,
+):
+    me = lax.axis_index("dp")
+    slot_count, chunks = patches_ref.shape[0], patches_ref.shape[1]
+    balanced = rows_ref.shape[0]
+    spare = stage.shape[2]
+    partners = [partner_of(me, q) for q in range(sections)]
+    count = counts_ref[me]
+    counts, leaving = [], []
+    for q in range(sections):
+        counts.append(count)
+        leaving.append(sends_ref[q, me])
+        count = count - sends_ref[q, me] + sends_ref[q, partners[q]]
+    greet_partners(me, sections)
+
+    def copies(q, k):
+        made = [
+            pltpu.make_async_remote_copy(
+                src_ref=stage.at[q, k], dst_ref=land.at[q, k],
+                send_sem=sent.at[q, k], recv_sem=landed.at[q, k],
+                device_id=(partners[q],), device_id_type=MESH,
+            )
+        ]
+        if k == 0:
+            made.append(
+                pltpu.make_async_remote_copy(
+                    src_ref=stage_tags.at[q], dst_ref=land_tags.at[q],
+                    send_sem=sent_tags.at[q], recv_sem=landed_tags.at[q],
+                    device_id=(partners[q],), device_id_type=MESH,
+                )
+            )
+        return made
+
+    def settle(q, k, source, arrived, target, limit):
+        for s in range(limit):
+            fresh = arrived[0]
+            for i in range(1, spare):
+                fresh = jnp.where(s - counts[q] >= i, arrived[i], fresh)
+            target(s, jnp.where(s < counts[q], source(s), fresh))
+
+    def finish(q, k):
+        for copy in copies(q, k):
+            copy.wait_recv()
+        last = q == sections - 1
+        limit = balanced if last else slot_count
+        blocks = patches_ref if q == 0 else slots
+        out = rows_ref if last else slots
+
+        def put(s, value):
+            out[s, k] = value
+
+        settle(q, k, lambda s: blocks[s, k], [land[q, k, i] for i in range(spare)], put, limit)
+        if k == 0:
+            tags = marks_ref if q == 0 else slot_tags
+            out_tags = tags_ref if last else slot_tags
+
+            def put_tags(s, value):
+                out_tags[s] = value
+
+            settle(q, k, lambda s: tags[s], [land_tags[q, i] for i in range(spare)], put_tags, limit)
+
+    def start(q, k):
+        blocks = patches_ref if q == 0 else slots
+        tags = marks_ref if q == 0 else slot_tags
+        for i in range(spare):
+            picked = jnp.clip(counts[q] - leaving[q] + i, 0, slot_count - 1)
+            stage[q, k, i] = blocks[picked, k]
+            if k == 0:
+                stage_tags[q, i] = tags[picked]
+        for copy in copies(q, k):
+            copy.start()
+
+    for t in range(chunks + 2 * (sections - 1)):
+        for q in range(sections):
+            k = t - 2 * q
+            if 0 <= k < chunks:
+                if q > 0:
+                    finish(q - 1, k)
+                start(q, k)
+    for k in range(chunks):
+        finish(sections - 1, k)
+    for q in range(sections):
+        for k in range(chunks):
+            for copy in copies(q, k):
+                copy.wait_send()
+
+
+def balance(patches, marks, block_counts, send_counts, balanced):
+    slot_count = marks.shape[0]
+    width = patches.shape[1]
+    sections = send_counts.shape[0]
+    spare = slot_count - balanced
+    rows = BLOCK // CHUNKS
+    vmem = pl.BlockSpec(memory_space=pltpu.VMEM)
+    smem = pl.BlockSpec(memory_space=pltpu.SMEM)
+    tag = marks.shape[1:]
+    return pl.pallas_call(
+        functools.partial(balance_kernel, sections),
+        out_shape=(
+            jax.ShapeDtypeStruct((balanced, CHUNKS, rows, width), patches.dtype),
+            jax.ShapeDtypeStruct((balanced,) + tag, marks.dtype),
+        ),
+        in_specs=[smem, smem, vmem, vmem],
+        out_specs=(vmem, vmem),
+        scratch_shapes=[
+            pltpu.VMEM((slot_count, CHUNKS, rows, width), patches.dtype),
+            pltpu.VMEM((slot_count,) + tag, marks.dtype),
+            pltpu.VMEM((sections, CHUNKS, spare, rows, width), patches.dtype),
+            pltpu.VMEM((sections, spare) + tag, marks.dtype),
+            pltpu.VMEM((sections, CHUNKS, spare, rows, width), patches.dtype),
+            pltpu.VMEM((sections, spare) + tag, marks.dtype),
+            pltpu.SemaphoreType.DMA((sections, CHUNKS)),
+            pltpu.SemaphoreType.DMA((sections, CHUNKS)),
+            pltpu.SemaphoreType.DMA((sections,)),
+            pltpu.SemaphoreType.DMA((sections,)),
+        ],
+        compiler_params=pltpu.CompilerParams(
+            collective_id=0, has_side_effects=True, vmem_limit_bytes=48 * 2**20
+        ),
+    )(block_counts, send_counts, patches.reshape(slot_count, CHUNKS, rows, width), marks)
+
+
+def reduce_kernel(orders, *refs):
+    parts = len(orders)
+    levels = len(orders[0])
+    ins, refs = refs[:parts], refs[parts:]
+    qkv_out, last_out = refs[0], refs[1]
+    scratch = refs[2:]
+    kept = [scratch[p * (levels + 1)] for p in range(parts)]
+    land = [scratch[p * (levels + 1) + 1:(p + 1) * (levels + 1)] for p in range(parts)]
+    sent, landed = scratch[-2], scratch[-1]
+    me = lax.axis_index("dp")
+    side = [(me // (1 << bit)) % 2 for bit in range(levels)]
+    greet_partners(me, levels)
+
+    def bases(p):
+        base, found = 0, [0]
+        for s in range(1, levels):
+            base = base + side[orders[p][s]] * (1 << (levels - 1 - s))
+            found.append(base)
+        return found
+
+    base_of = [bases(p) for p in range(parts)]
+
+    def copy_of(p, s):
+        bit = orders[p][s]
+        if s == 0:
+            source = ins[p].at[:, 1 - side[0]]
+        else:
+            half = 1 << (levels - 1 - s)
+            source = kept[p].at[
+                pl.ds(base_of[p][s - 1] + (1 - side[bit]) * half, half)
+            ]
+        return pltpu.make_async_remote_copy(
+            src_ref=source, dst_ref=land[p][s],
+            send_sem=sent.at[p, s], recv_sem=landed.at[p, s],
+            device_id=(partner_of(me, bit),), device_id_type=MESH,
+        )
+
+    def add(p, s):
+        total = 1 << (levels - 1 - s)
+        if s == 0:
+
+            def step(j, carry):
+                chip = 0
+                for i in range(1, levels):
+                    chip = chip + ((j // (1 << (levels - 1 - i))) % 2) * (1 << (orders[p][i] - 1))
+                kept[p][j] = (
+                    ins[p][chip, side[0]].astype(jnp.float32) + land[p][0][chip].astype(jnp.float32)
+                ).astype(jnp.bfloat16)
+                return carry
+
+            lax.fori_loop(0, total, step, 0)
+            return
+        own = base_of[p][s]
+        if s < levels - 1:
+
+            def step(j, carry):
+                kept[p][own + j] = (
+                    kept[p][own + j].astype(jnp.float32) + land[p][s][j].astype(jnp.float32)
+                ).astype(jnp.bfloat16)
+                return carry
+
+            lax.fori_loop(0, total, step, 0)
+            return
+        final = kept[p][own].astype(jnp.float32) + land[p][s][0].astype(jnp.float32)
+        if p < parts - 1:
+            width = final.shape[1]
+            qkv_out[:, p * width:(p + 1) * width] = final
+        else:
+            last_out[...] = final
+
+    for s in range(levels + 1):
+        for p in range(parts):
+            if s > 0:
+                copy_of(p, s - 1).wait_recv()
+                add(p, s - 1)
+            if s < levels:
+                copy_of(p, s).start()
+    for p in range(parts):
+        for s in range(levels):
+            copy_of(p, s).wait_send()
+
+
+def reduce_rows(parts, devices):
+    levels = devices.bit_length() - 1
+    bits = list(range(1, levels))
+    orders = []
+    for p in range(len(parts)):
+        first = bits[:3]
+        turn = p % len(first)
+        orders.append([0] + first[turn:] + first[:turn] + bits[3:])
+    shaped = [
+        part.reshape(devices // 2, 2, part.shape[0] // devices, part.shape[1]) for part in parts
+    ]
+    vmem = pl.BlockSpec(memory_space=pltpu.VMEM)
+    scratch = []
+    for part in shaped:
+        scratch.append(pltpu.VMEM((devices // 2,) + part.shape[2:], jnp.bfloat16))
+        for s in range(levels):
+            scratch.append(pltpu.VMEM((1 << (levels - 1 - s),) + part.shape[2:], jnp.bfloat16))
+    count = len(parts)
+    scratch += [pltpu.SemaphoreType.DMA((count, levels))] * 2
+    qkv, last = shaped[0].shape, shaped[-1].shape
+    return pl.pallas_call(
+        functools.partial(reduce_kernel, orders),
+        out_shape=(
+            jax.ShapeDtypeStruct((qkv[2], (count - 1) * qkv[3]), jnp.float32),
+            jax.ShapeDtypeStruct(last[2:], jnp.float32),
+        ),
+        in_specs=[vmem] * count,
+        out_specs=(vmem, vmem),
+        scratch_shapes=scratch,
+        compiler_params=pltpu.CompilerParams(
+            collective_id=1, has_side_effects=True, vmem_limit_bytes=56 * 2**20
+        ),
+    )(*shaped)
 
 
 def token_layout(patch_grids):
@@ -35,21 +289,6 @@
     row_index = offset // span
     col_index = offset - row_index * span
     return (segment, row_index, col_index, in_image)
-
-
-def embed_blocks(patch_rows, patch_grids, row_table, col_table):
-    block_total = patch_grids.shape[0]
-    segment, row_index, col_index, in_image = token_layout(patch_grids)
-    levels = jnp.arange(row_table.shape[0], dtype=jnp.int32)
-    row_hot = (row_index.reshape(-1, 1) == levels[None, :]).astype(jnp.bfloat16)
-    col_hot = (col_index.reshape(-1, 1) == levels[None, :]).astype(jnp.bfloat16)
-    table_sum = jnp.dot(row_hot, row_table, preferred_element_type=jnp.float32) + jnp.dot(
-        col_hot, col_table, preferred_element_type=jnp.float32
-    )
-    embedded = (
-        patch_rows.astype(jnp.float32) + table_sum * in_image.reshape(-1, 1).astype(jnp.float32)
-    ).astype(jnp.bfloat16)
-    return (embedded.reshape(block_total, BLOCK, patch_rows.shape[1]), segment)
 
 
 def layer_forward(blocks, marks, ln_gain, ln_bias, w_qkv, b_qkv, w_out, b_out):
@@ -107,12 +346,14 @@
     query_grad = jnp.einsum("bhqk,bkhd->bqhd", score_grad, key_f)
     key_grad = jnp.einsum("bhqk,bqhd->bkhd", score_grad, query_f)
     row_total = query_f.shape[0] * query_f.shape[1]
-    mixed_grad = (
-        jnp.stack([query_grad, key_grad, value_grad], axis=2)
-        .reshape(row_total, -1)
-        .astype(jnp.bfloat16)
-    )
-    return jnp.dot(normed.T, mixed_grad, preferred_element_type=jnp.float32)
+    return [
+        jnp.dot(
+            normed.T,
+            part.reshape(row_total, -1).astype(jnp.bfloat16),
+            preferred_element_type=jnp.float32,
+        ).astype(jnp.bfloat16)
+        for part in (query_grad, key_grad, value_grad)
+    ]
 
 
 def local(
@@ -130,50 +371,31 @@
     b_out,
     cotangent,
 ):
-    slot_count = patches.shape[0] // BLOCK
     balanced = cotangent.shape[0] // BLOCK
-    spare_slots = slot_count - balanced
-    embedded, segment = embed_blocks(patches, patch_grids, row_table, col_table)
-    segment_marks = segment.astype(jnp.bfloat16)
-    all_ranks = jnp.arange(block_counts.shape[0], dtype=jnp.int32)
+    width = patches.shape[1]
+    devices = lax.axis_size("dp")
     own_rank = lax.axis_index("dp")
-    counts = block_counts
-    slot_ids = jnp.arange(slot_count, dtype=jnp.int32)
-    section_total = lax.axis_size("dp").bit_length() - 1
-    for section_index in range(section_total):
-        partner = jnp.bitwise_xor(all_ranks, 1 << section_index)
-        sent_now = send_counts[section_index]
-        received = sent_now[partner]
-        own_count = counts[own_rank]
-        leaving = sent_now[own_rank]
-        arriving = received[own_rank]
-        staying = slot_ids < own_count - leaving
-        landing = (slot_ids >= own_count) & (slot_ids < own_count + arriving)
-        picked = jnp.clip(
-            own_count - leaving + jnp.arange(spare_slots, dtype=jnp.int32), 0, slot_count - 1
-        )
-        far_blocks, far_marks = partner_2(
-            (jnp.take(embedded, picked, axis=0), jnp.take(segment_marks, picked, axis=0)),
-            "dp",
-            section_index,
-        )
-        source = jnp.clip(slot_ids - own_count, 0, spare_slots - 1)
-        arrived = jnp.take(far_blocks, source, axis=0)
-        arrived_marks = jnp.take(far_marks, source, axis=0)
-        embedded = jnp.where(
-            staying[:, None, None],
-            embedded,
-            jnp.where(landing[:, None, None], arrived, jnp.zeros_like(embedded)),
-        )
-        segment_marks = jnp.where(
-            staying[:, None],
-            segment_marks,
-            jnp.where(landing[:, None], arrived_marks, -jnp.ones_like(segment_marks)),
-        )
-        counts = counts - sent_now + received
-    live_count = counts[own_rank]
-    rank_blocks = embedded[:balanced]
-    rank_marks = segment_marks[:balanced]
+    segment, row_index, col_index, in_image = token_layout(patch_grids)
+    marks = jnp.stack([segment, row_index, col_index, in_image], axis=1).astype(jnp.float32)
+    marks = jnp.pad(marks, ((0, 0), (0, 8 - marks.shape[1]), (0, 0)))
+    rows, tags = balance(patches, marks, block_counts, send_counts, balanced)
+    live_count = block_counts[own_rank]
+    for section in range(send_counts.shape[0]):
+        sent_now = send_counts[section]
+        live_count = live_count - sent_now[own_rank] + sent_now[own_rank ^ (1 << section)]
+    rank_marks = tags[:, 0]
+    levels = jnp.arange(row_table.shape[0], dtype=jnp.float32)
+    here = tags[:, 3].reshape(-1, 1) > 0
+    row_hot = (here & (tags[:, 1].reshape(-1, 1) == levels)).astype(jnp.bfloat16)
+    col_hot = (here & (tags[:, 2].reshape(-1, 1) == levels)).astype(jnp.bfloat16)
+    table_sum = jnp.dot(row_hot, row_table, preferred_element_type=jnp.float32) + jnp.dot(
+        col_hot, col_table, preferred_element_type=jnp.float32
+    )
+    rank_blocks = (
+        (rows.reshape(-1, width).astype(jnp.float32) + table_sum)
+        .astype(jnp.bfloat16)
+        .reshape(balanced, BLOCK, width)
+    )
     rank_live = jnp.arange(balanced, dtype=jnp.int32) < live_count
     result, saved = layer_forward(
         rank_blocks, rank_marks, ln_gain, ln_bias, w_qkv, b_qkv, w_out, b_out
@@ -183,11 +405,8 @@
     token_live = (rank_live[:, None] & (rank_marks >= 0)).reshape(-1, 1)
     out_grad = jnp.where(token_live, cotangent, jnp.zeros_like(cotangent))
     grad_out, attn_grad = output_backward(out_grad, saved, w_out)
-    grad_qkv = qkv_backward(attn_grad, saved)
-    qkv_rows, out_rows = (
-        lax.psum_scatter(grad_qkv, "dp", scatter_dimension=0, tiled=True),
-        lax.psum_scatter(grad_out, "dp", scatter_dimension=0, tiled=True),
-    )
+    parts = qkv_backward(attn_grad, saved) + [grad_out.astype(jnp.bfloat16)]
+    qkv_rows, out_rows = reduce_rows(parts, devices)
     return (result, qkv_rows, out_rows)
 
 

time: 369 us -> 175 us (0.47)
  Pallas kernels: 0 us -> 98.5 us
  blocking collectives: 92.3 us -> 0 us
  waiting for transfers between devices: 90.6 us -> 0 us
  local copies, waits for them, and re-layouts: 69.2 us -> 33.5 us
  other arithmetic: 28.2 us -> 3.96 us
  starting transfers between devices: 23.4 us -> 0 us
  between operations: 27.3 us -> 7.93 us
  matrix products: 36.3 us -> 30.5 us
    pallas_call x0 -> x2, Pallas kernels: none -> 98.5 us  [the longest x1 50.5 us: balance(): pl.pallas_call(functools.partial(balance_kernel, sections), out_shape=(ja...]
    unnamed x1 -> x0, blocking collectives: 92.3 us -> none
    ppermute x10 -> x0, waiting for transfers between devices: 54 us -> none  [partner_2(): lax.ppermute(value, axis, [(i, i ^ 1 << stride) for i in range(lax.axis_s...]
    unnamed x8 -> x0, waiting for transfers between devices: 36.5 us -> none
    gather x25 -> x0, local copies, waits for them, and re-layouts: 29.9 us -> none  [the longest x5 10.7 us: local(): jnp.take(embedded, picked, axis=0)]
    select_n x34 -> x0, other arithmetic: 19.5 us -> none  [the longest x4 14.9 us: local(): jnp.where(staying[:, None, None], embedded, jnp.where(landing[:, None, No...]
    ppermute x10 -> x0, starting transfers between devices: 15 us -> none  [partner_2(): lax.ppermute(value, axis, [(i, i ^ 1 << stride) for i in range(lax.axis_s...]
    unnamed x7 -> x0, starting transfers between devices: 8.46 us -> none
  transfers between devices with their start and end apart: 17 -> 0, of which waited for: 7 -> 0; matrix products, arithmetic and copies ran while one was open for 41% -> 0% of each run, Pallas kernels for 0% -> 0%
where the time goes in v1:
time: 175 us; the launch traced here: 174 us
  Pallas kernels  98.5 us (56%)
  local copies, waits for them, and re-layouts  33.5 us (19%)
  matrix products  30.5 us (17%)
  between operations  7.93 us (5%)
  other arithmetic  3.96 us (2%)
    pallas_call x1, Pallas kernels, balance(): pl.pallas_call(functools.partial(balance_kernel, sections), out_shape=(ja...  50.5 us
    pallas_call x1, Pallas kernels, reduce_rows(): pl.pallas_call(functools.partial(reduce_kernel, orders), out_shape=(jax.S...  48 us
    unnamed x33, local copies, waits for them, and re-layouts  12.6 us
    dot_general x3, matrix products, qkv_backward(): jnp.dot(normed.T, part.reshape(row_total, -1).astype(jnp.bfloat16), prefe...  8.43 us
    dot_general x1, matrix products, layer_forward(): jnp.dot(normed, w_qkv, preferred_element_type=jnp.float32)  6.71 us
    reshape x1, local copies, waits for them, and re-layouts, layer_forward(): mixed.reshape(block_total, BLOCK, 3, head_count, HEAD).astype(jnp.float32)  6.42 us

profile of v1, /device:TPU:0, one launch (start us, length us, event | category | flops | bytes accessed | tf_op | source)
XLA Modules:
  0.0 174.5 jit_solution(7441039441105709917)
XLA Ops:
  0.7 1.4 dynamic_slice.33
  2.0 0.9 fusion.76
  2.9 0.7 constant_dynamic-slice_fusion
  11.9 0.8 fusion.77
  13.4 0.7 convert_element_type.103
  14.1 0.7 convert_element_type.104
  14.8 0.7 convert_element_type.106
  15.5 0.7 convert_element_type.112
  16.2 1.5 copy-done.1
  17.8 0.7 copy-done.2
  19.1 50.5 %shard_map.148 = (bf16[4,8,16,1280]{3,2,1,0:T(8,128)(2,1)S(1)}, f32[4,8,128]{2,1,0:T(8,128)S(1)}) custom-call(s32[32]{0:T(128)S(1)} %copy-done.3, s32[5,32]{1,0:T(8,128)S(1)} %copy-done.2, bf16[6,8,16,1280]{3,2,1,0:T(8,128)(2,1)S(1)} %bitcast.106, f32[6,8,128]{2,1,0:T(8,128)S(1)} %pad.4.marks_ref), custom_call_target="tpu_custom_call" | custom-call | tf_op jit(solution)/shard_map/pallas_call | solution.py:130
  69.9 2.0 %fusion.39 = bf16[512,640]{0,1:T(8,128)(2,1)} fusion(bf16[640,1280]{1,0:T(8,128)(2,1)S(1)} %copy-done, bf16[512,1280]{1,0:T(8,128)(2,1)S(1)} %copy-done.11, pred[512]{0:T(512)(128)(4,1)S(1)} %bitcast_and_fusion), kind=kOutput, calls=%fused_computation.59 | convolution fusion | flops 839516160 | bytes 3604992 | tf_op jit(solution)/shard_map/dot_general | solution.py:334
  71.8 2.4 %reshape.217 = bf16[4,128,8,80]{1,0,3,2:T(4,128)(2,1)} reshape(bf16[512,640]{0,1:T(8,128)(2,1)} %fusion.39) | data formatting | bytes 1310720 | tf_op jit(solution)/shard_map/reshape | solution.py:335
  74.8 0.8 convert_reduce_fusion
  76.7 6.7 %add_convert_fusion = bf16[512,1920]{1,0:T(8,128)(2,1)} fusion(bf16[1280,1920]{1,0:T(8,128)(2,1)} %param.21, f32[1920]{0:T(1024)S(1)} %convert_element_type.106, bf16[512,1280]{1,0:T(8,128)(2,1)S(1)} %get-tuple-element.44, f32[1280]{0:T(1024)S(1)} %convert_element_type.104, f32[1280]{0:T(1024)S(1)} %convert_element_type.103, f32[512]{0:T(512)S(1)} %add_rsqrt_fusion, ...), kind=kOutput, calls=%fused_computation.1 | convolution fusion | flops 2522480640 | bytes 8214016 | tf_op jit(solution)/shard_map/dot_general | solution.py:308
  83.4 6.4 %reshape.223 = bf16[4,128,3,8,80]{4,3,2,1,0:T(8,128)(2,1)} reshape(bf16[512,1920]{1,0:T(8,128)(2,1)} %add_convert_fusion) | data formatting | bytes 3932160 | tf_op jit(solution)/shard_map/reshape | solution.py:310
  89.8 3.4 %fusion.74 = (bf16[4,128,1,8,80]{4,3,2,1,0:T(8,128)(2,1)}, bf16[4,128,1,8,80]{4,3,2,1,0:T(8,128)(2,1)}, bf16[4,128,1,8,80]{4,3,2,1,0:T(8,128)(2,1)S(1)}) fusion(bf16[4,128,3,8,80]{4,3,2,1,0:T(8,128)(2,1)} %reshape.223), kind=kLoop, calls=%fused_computation.108 | loop fusion | bytes 3932160 | tf_op jit(solution)/shard_map/slice | solution.py:311
  93.2 1.6 copy.72
  94.9 2.3 %copy.71 = bf16[4,128,1,8,80]{1,4,3,0,2:T(8,128)(2,1)} copy(bf16[4,128,1,8,80]{4,3,2,1,0:T(8,128)(2,1)} %get-tuple-element.20) | data formatting | bytes 1310720
  97.2 1.4 copy.73
  98.6 3.4 %fusion.78 = (f32[4,8,128]{2,1,0:T(8,128)S(1)}, f32[4,8,128,128]{2,3,1,0:T(8,128)}) fusion(pred[4,128,128]{1,2,0:T(8,128)(4,1)S(1)} %broadcast_compare_fusion, bf16[4,128,1,8,80]{1,4,3,0,2:T(8,128)(2,1)} %copy.73, bf16[4,128,1,8,80]{1,4,3,0,2:T(8,128)(2,1)S(1)} %copy.72), kind=kOutput, calls=%fused_computation.112 | convolution fusion | flops 85983360 | bytes 3489792 | tf_op jit(solution)/shard_map/sub | solution.py:319
  102.0 2.6 %fusion.15 = bf16[4,128,8,80]{1,3,2,0:T(8,128)(2,1)S(1)} fusion(bf16[4,128,8,80]{1,0,3,2:T(4,128)(2,1)S(1)} %copy-done.6, f32[4,8,128,128]{2,3,1,0:T(8,128)} %get-tuple-element.46, f32[4,8,128]{2,1,0:T(8,128)S(1)} %get-tuple-element.45), kind=kOutput, calls=%fused_computation.34 | convolution fusion | flops 84934656 | bytes 3424256 | tf_op jit(solution)/shard_map/bhqk,bqhd->bkhd/dot_general | solution.py:342
  106.8 0.9 fusion.14
  109.7 2.8 %convolution_convert_fusion.2 = bf16[1280,640]{1,0:T(8,128)(2,1)} fusion(bf16[80,8,4,128]{3,2,1,0:T(4,128)(2,1)S(1)} %bitcast.115, bf16[512,1280]{1,0:T(8,128)(2,1)S(1)} %copy-done.5, f32[1280]{0:T(1024)S(1)} %convert_element_type.104, f32[1280]{0:T(1024)S(1)} %convert_element_type.103, f32[512]{0:T(512)S(1)} %add_rsqrt_fusion, ...), kind=kOutput, calls=%fused_computation.10 | convolution fusion | flops 843612160 | bytes 3618816 | tf_op jit(solution)/shard_map/dot_general | solution.py:350
  112.5 2.8 %convolution_convert_fusion.3 = bf16[1280,640]{1,0:T(8,128)(2,1)} fusion(bf16[80,8,4,128]{3,2,1,0:T(4,128)(2,1)S(1)} %bitcast.114, bf16[512,1280]{1,0:T(8,128)(2,1)S(1)} %copy-done.5, f32[1280]{0:T(1024)S(1)} %convert_element_type.104, f32[1280]{0:T(1024)S(1)} %convert_element_type.103, f32[512]{0:T(512)S(1)} %add_rsqrt_fusion, ...), kind=kOutput, calls=%fused_computation.11 | convolution fusion | flops 843612160 | bytes 3618816 | tf_op jit(solution)/shard_map/dot_general | solution.py:350
  115.3 2.8 %convolution_convert_fusion.1 = bf16[1280,640]{1,0:T(8,128)(2,1)} fusion(bf16[80,8,4,128]{3,2,1,0:T(4,128)(2,1)S(1)} %bitcast.113, bf16[512,1280]{1,0:T(8,128)(2,1)S(1)} %copy-done.5, f32[1280]{0:T(1024)S(1)} %convert_element_type.104, f32[1280]{0:T(1024)S(1)} %convert_element_type.103, f32[512]{0:T(512)S(1)} %add_rsqrt_fusion, ...), kind=kOutput, calls=%fused_computation.9 | convolution fusion | flops 843612160 | bytes 3618816 | tf_op jit(solution)/shard_map/dot_general | solution.py:350
  118.1 2.4 %fusion.6 = bf16[512,1280]{1,0:T(8,128)(2,1)} fusion(bf16[640,1280]{1,0:T(8,128)(2,1)S(1)} %copy-done, bf16[512,1280]{1,0:T(8,128)(2,1)S(1)} %copy-done.5, f32[1280]{0:T(1024)S(1)} %convert_element_type.112, pred[512]{0:T(512)(128)(4,1)S(1)} %broadcast_bitcast_fusion, bf16[80,8,4,128]{3,2,1,0:T(4,128)(2,1)S(1)} %bitcast.111), kind=kOutput, calls=%fused_computation.16 | convolution fusion | flops 842137600 | bytes 4920832 | tf_op jit(solution)/shard_map/dot_general | solution.py:324
  120.5 1.1 convolution_convert_fusion
  121.7 1.5 reshape.221.refs_3_
  123.1 48.0 %shard_map.149 = (f32[40,1920]{1,0:T(8,128)}, f32[20,1280]{1,0:T(8,128)}) custom-call(bf16[16,2,40,640]{3,2,1,0:T(8,128)(2,1)} %bitcast.109, bf16[16,2,40,640]{3,2,1,0:T(8,128)(2,1)} %bitcast.108, bf16[16,2,40,640]{3,2,1,0:T(8,128)(2,1)} %bitcast.110, bf16[16,2,20,1280]{3,2,1,0:T(8,128)(2,1)} %reshape.221.refs_3_), custom_call_target="tpu_custom_call" | custom-call | tf_op jit(solution)/shard_map/pallas_call | solution.py:258
  171.2 1.7 copy.106
  172.9 1.6 copy.107
  (57 shorter events, 8.8 us)
Async XLA Ops:
  0.6 69.2 %copy-start = (bf16[640,1280]{1,0:T(8,128)(2,1)S(1)}, bf16[640,1280]{1,0:T(8,128)(2,1)}, u32[]{:S(2)}) copy-start(bf16[640,1280]{1,0:T(8,128)(2,1)} %param.23) | copy-start | bytes 4915204
  16.2 1.5 copy-start.1
  17.8 0.7 copy-start.2
  18.4 0.7 copy-start.3
  19.1 50.8 %copy-start.11 = (bf16[512,1280]{1,0:T(8,128)(2,1)S(1)}, bf16[512,1280]{1,0:T(8,128)(2,1)}, u32[]{:S(2)}) copy-start(bf16[512,1280]{1,0:T(8,128)(2,1)} %param.25) | copy-start | bytes 3932164
  69.9 4.3 %copy-start.10 = (bf16[16,1280]{1,0:T(8,128)(2,1)S(1)}, bf16[16,1280]{1,0:T(8,128)(2,1)}, u32[]{:S(2)}) copy-start(bf16[16,1280]{1,0:T(8,128)(2,1)} %param.17) | copy-start | bytes 122884
  71.8 3.0 %copy-start.9 = (bf16[16,1280]{1,0:T(8,128)(2,1)S(1)}, bf16[16,1280]{1,0:T(8,128)(2,1)}, u32[]{:S(2)}) copy-start(bf16[16,1280]{1,0:T(8,128)(2,1)} %param.18) | copy-start | bytes 122884
  75.6 1.1 copy-start.4
  98.6 3.4 %copy-start.6 = (bf16[4,128,8,80]{1,0,3,2:T(4,128)(2,1)S(1)}, bf16[4,128,8,80]{1,0,3,2:T(4,128)(2,1)}, u32[]{:S(2)}) copy-start(bf16[4,128,8,80]{1,0,3,2:T(4,128)(2,1)} %reshape.217) | copy-start | bytes 1966084
  102.0 3.1 %copy-start.8 = (bf16[4,128,1,8,80]{1,4,3,0,2:T(8,128)(2,1)S(1)}, bf16[4,128,1,8,80]{1,4,3,0,2:T(8,128)(2,1)}, u32[]{:S(2)}) copy-start(bf16[4,128,1,8,80]{1,4,3,0,2:T(8,128)(2,1)} %copy.71) | copy-start | bytes 1966084
  102.0 3.1 %copy-start.13 = (f32[4,8,128,128]{2,3,1,0:T(8,128)S(1)}, f32[4,8,128,128]{2,3,1,0:T(8,128)}, u32[]{:S(2)}) copy-start(f32[4,8,128,128]{2,3,1,0:T(8,128)} %get-tuple-element.46) | copy-start | bytes 6291460
  106.8 1.1 copy-start.7
  108.4 1.3 copy-start.5
  118.1 2.4 %copy-start.12 = (bf16[512,1280]{1,0:T(8,128)(2,1)S(1)}, bf16[512,1280]{1,0:T(8,128)(2,1)}, u32[]{:S(2)}) copy-start(bf16[512,1280]{1,0:T(8,128)(2,1)} %param.25) | copy-start | bytes 3932164

commit v2 on v1

--- a/solution.py
+++ b/solution.py
@@ -88,7 +88,11 @@
             out_tags = tags_ref if last else slot_tags
 
             def put_tags(s, value):
-                out_tags[s] = value
+                if last:
+                    out_tags[s, :8] = value
+                    out_tags[s, 8:] = jnp.full(value.shape, jnp.where(s < count, 1.0, 0.0))
+                else:
+                    out_tags[s] = value
 
             settle(q, k, lambda s: tags[s], [land_tags[q, i] for i in range(spare)], put_tags, limit)
 
@@ -131,7 +135,7 @@
         functools.partial(balance_kernel, sections),
         out_shape=(
             jax.ShapeDtypeStruct((balanced, CHUNKS, rows, width), patches.dtype),
-            jax.ShapeDtypeStruct((balanced,) + tag, marks.dtype),
+            jax.ShapeDtypeStruct((balanced, 2 * tag[0], tag[1]), marks.dtype),
         ),
         in_specs=[smem, smem, vmem, vmem],
         out_specs=(vmem, vmem),
@@ -270,90 +274,173 @@
     )(*shaped)
 
 
-def token_layout(patch_grids):
-    heights = patch_grids[:, :, 0]
-    widths = patch_grids[:, :, 1]
-    image_area = heights * widths
-    image_end = jnp.cumsum(image_area, axis=1)
-    image_start = image_end - image_area
-    positions = jnp.arange(BLOCK, dtype=jnp.int32)[None, :, None]
-    member = ((positions >= image_start[:, None, :]) & (positions < image_end[:, None, :])).astype(
-        jnp.int32
+def dot(a, b, dims=((1,), (0,))):
+    return lax.dot_general(a, b, (dims, ((), ())), preferred_element_type=jnp.float32)
+
+
+ROWS = ((0,), (0,))
+COLS = ((1,), (1,))
+
+
+def block_layout(tags, images, levels):
+    position = lax.broadcasted_iota(jnp.int32, (1, BLOCK), 1).astype(jnp.float32)
+    start = jnp.zeros((1, BLOCK), jnp.float32)
+    segment = jnp.full((1, BLOCK), -1.0, jnp.float32)
+    offset = jnp.zeros((1, BLOCK), jnp.float32)
+    span = jnp.ones((1, BLOCK), jnp.float32)
+    for j in range(images):
+        columns = tags[2 * j + 1:2 * j + 2]
+        end = start + tags[2 * j:2 * j + 1] * columns
+        member = (position >= start) & (position < end)
+        segment = jnp.where(member, float(j), segment)
+        offset = jnp.where(member, position - start, offset)
+        span = jnp.where(member, columns, span)
+        start = end
+    row = jnp.floor((offset + 0.5) / span)
+    col = offset - row * span
+    inside = segment >= 0.0
+    level = lax.broadcasted_iota(jnp.int32, (2 * levels, BLOCK), 0).astype(jnp.float32)
+    wanted = jnp.where(level < levels, row, col + levels)
+    hot = jnp.where((level == wanted) & inside, 1.0, 0.0).astype(jnp.bfloat16)
+    kind = lax.broadcasted_iota(jnp.int32, (8, BLOCK), 0).astype(jnp.float32) - 1.0
+    kinds = jnp.where(kind == segment, 1.0, 0.0).astype(jnp.bfloat16)
+    return hot, kinds, inside
+
+
+def layer_kernel(
+    images, patches_ref, tags_ref, row_ref, col_ref, gain_ref, bias_ref, w_qkv_ref, b_qkv_ref,
+    w_out_ref, b_out_ref, cot_ref, out_ref, gq_ref, gk_ref, gv_ref, go_ref,
+    x_s, normed_s, grad_s, qkv_s, ag_s, att_s, dqkv_s, same_s,
+):
+    blocks = patches_ref.shape[0]
+    inner, width = w_out_ref.shape
+    heads = inner // HEAD
+    rows_total = blocks * BLOCK
+    levels = row_ref.shape[0]
+    tables = jnp.concatenate([row_ref[...], col_ref[...]], axis=0)
+    scale = 1.0 / math.sqrt(HEAD)
+
+    def embed(b, carry):
+        rows = pl.ds(pl.multiple_of(b * BLOCK, BLOCK), BLOCK)
+        tags = tags_ref[b]
+        hot, kinds, inside = block_layout(tags, images, levels)
+        live = tags[8:9]
+        same_s[b] = dot(kinds, kinds, ROWS)
+        wanted = jnp.where(inside, live, 0.0)
+        first = lax.broadcasted_iota(jnp.int32, (8, BLOCK), 0) == 0
+        wanted = jnp.where(first, wanted, 0.0).astype(jnp.bfloat16)
+        keep = dot(wanted, jnp.ones((8, BLOCK), jnp.bfloat16), ROWS)[:, :1]
+        grad_s[rows, :] = jnp.where(keep > 0.5, cot_ref[rows, :].astype(jnp.float32), 0.0).astype(
+            jnp.bfloat16
+        )
+        x = (patches_ref[b].astype(jnp.float32) + dot(hot, tables, ROWS)).astype(jnp.bfloat16)
+        x_s[rows, :] = x
+        x = x.astype(jnp.float32)
+        centred = x - jnp.mean(x, axis=-1, keepdims=True)
+        variance = jnp.mean(centred * centred, axis=-1, keepdims=True)
+        normed_s[rows, :] = (
+            centred * lax.rsqrt(variance + EPSILON) * gain_ref[...].astype(jnp.float32)
+            + bias_ref[...].astype(jnp.float32)
+        ).astype(jnp.bfloat16)
+        return carry
+
+    lax.fori_loop(0, blocks, embed, 0)
+    for p in range(3):
+        part = slice(p * inner, (p + 1) * inner)
+        qkv_s[:, part] = (
+            dot(normed_s[...], w_qkv_ref[:, part]) + b_qkv_ref[:, part].astype(jnp.float32)
+        ).astype(jnp.bfloat16)
+    ag_s[...] = dot(grad_s[...], w_out_ref[...], COLS).astype(jnp.bfloat16)
+
+    def attend(b, carry):
+        rows = pl.ds(pl.multiple_of(b * BLOCK, BLOCK), BLOCK)
+        same = same_s[b] > 0.5
+        qkv = qkv_s[rows, :]
+        outer = ag_s[rows, :]
+        found = [[], [], [], []]
+        for h in range(heads):
+            part = [qkv[:, p * inner + h * HEAD:p * inner + (h + 1) * HEAD] for p in range(3)]
+            query, key, value = part
+            given = outer[:, h * HEAD:(h + 1) * HEAD]
+            scores = jnp.where(same, dot(query, key, COLS) * scale, -1e30)
+            expo = jnp.exp(scores - jnp.max(scores, axis=-1, keepdims=True))
+            probs = expo / jnp.sum(expo, axis=-1, keepdims=True)
+            probs_b = probs.astype(jnp.bfloat16)
+            found[3].append(dot(probs_b, value).astype(jnp.bfloat16))
+            prob_grad = dot(given, value, COLS)
+            score_grad = (
+                probs * (prob_grad - jnp.sum(prob_grad * probs, axis=-1, keepdims=True)) * scale
+            ).astype(jnp.bfloat16)
+            found[0].append(dot(score_grad, key).astype(jnp.bfloat16))
+            found[1].append(dot(score_grad, query, ROWS).astype(jnp.bfloat16))
+            found[2].append(dot(probs_b, given, ROWS).astype(jnp.bfloat16))
+        for p in range(3):
+            dqkv_s[rows, p * inner:(p + 1) * inner] = jnp.concatenate(found[p], axis=1)
+        att_s[rows, :] = jnp.concatenate(found[3], axis=1)
+        return carry
+
+    lax.fori_loop(0, blocks, attend, 0)
+
+    def project(b, carry):
+        rows = pl.ds(pl.multiple_of(b * BLOCK, BLOCK), BLOCK)
+        live = jnp.concatenate([tags_ref[b][8:9]] * (width // BLOCK), axis=1)
+        projected = dot(att_s[rows, :], w_out_ref[...]) + b_out_ref[...].astype(jnp.float32)
+        total = x_s[rows, :].astype(jnp.float32) + projected
+        out_ref[rows, :] = jnp.where(live > 0.5, total, 0.0).astype(jnp.bfloat16)
+        return carry
+
+    lax.fori_loop(0, blocks, project, 0)
+    tile = 2 * BLOCK
+
+    def weigh(i, carry):
+        rows = pl.ds(pl.multiple_of(i * tile, tile), tile)
+        for p, target in enumerate((gq_ref, gk_ref, gv_ref)):
+            target[rows, :] = dot(
+                normed_s[:, rows], dqkv_s[:, p * inner:(p + 1) * inner], ROWS
+            ).astype(jnp.bfloat16)
+        return carry
+
+    lax.fori_loop(0, width // tile, weigh, 0)
+
+    def weigh_out(i, carry):
+        rows = pl.ds(pl.multiple_of(i * BLOCK, BLOCK), BLOCK)
+        go_ref[rows, :] = dot(att_s[:, rows], grad_s[...], ROWS).astype(jnp.bfloat16)
+        return carry
+
+    lax.fori_loop(0, inner // BLOCK, weigh_out, 0)
+
+
+def layer(images, patches, tags, row_table, col_table, gain, bias, w_qkv, b_qkv, w_out, b_out, cot):
+    rows, width = cot.shape
+    inner = w_out.shape[0]
+    vmem = pl.BlockSpec(memory_space=pltpu.VMEM)
+    half = jnp.bfloat16
+    return pl.pallas_call(
+        functools.partial(layer_kernel, images),
+        out_shape=(
+            jax.ShapeDtypeStruct((rows, width), half),
+            jax.ShapeDtypeStruct((width, inner), half),
+            jax.ShapeDtypeStruct((width, inner), half),
+            jax.ShapeDtypeStruct((width, inner), half),
+            jax.ShapeDtypeStruct((inner, width), half),
+        ),
+        in_specs=[vmem] * 11,
+        out_specs=(vmem,) * 5,
+        scratch_shapes=[
+            pltpu.VMEM((rows, width), half),
+            pltpu.VMEM((rows, width), half),
+            pltpu.VMEM((rows, width), half),
+            pltpu.VMEM((rows, 3 * inner), half),
+            pltpu.VMEM((rows, inner), half),
+            pltpu.VMEM((rows, inner), half),
+            pltpu.VMEM((rows, 3 * inner), half),
+            pltpu.VMEM((rows // BLOCK, BLOCK, BLOCK), jnp.float32),
+        ],
+        compiler_params=pltpu.CompilerParams(vmem_limit_bytes=56 * 2**20),
+    )(
+        patches, tags, row_table, col_table, gain.reshape(1, -1), bias.reshape(1, -1),
+        w_qkv, b_qkv.reshape(1, -1), w_out, b_out.reshape(1, -1), cot,
     )
-    image_ids = jnp.arange(patch_grids.shape[1], dtype=jnp.int32)
-    in_image = jnp.sum(member, axis=-1)
-    segment = jnp.sum(member * image_ids, axis=-1) + in_image - 1
-    offset = positions[:, :, 0] - jnp.sum(member * image_start[:, None, :], axis=-1)
-    offset = offset * in_image
-    span = jnp.maximum(jnp.sum(member * widths[:, None, :], axis=-1), 1)
-    row_index = offset // span
-    col_index = offset - row_index * span
-    return (segment, row_index, col_index, in_image)
-
-
-def layer_forward(blocks, marks, ln_gain, ln_bias, w_qkv, b_qkv, w_out, b_out):
-    block_total = blocks.shape[0]
-    model_width = blocks.shape[2]
-    inner = w_out.shape[0]
-    head_count = inner // HEAD
-    rows = blocks.reshape(block_total * BLOCK, model_width).astype(jnp.float32)
-    average = jnp.mean(rows, axis=-1, keepdims=True)
-    centred = rows - average
-    variance = jnp.mean(centred * centred, axis=-1, keepdims=True)
-    normed = (
-        centred * lax.rsqrt(variance + EPSILON) * ln_gain.astype(jnp.float32)
-        + ln_bias.astype(jnp.float32)
-    ).astype(jnp.bfloat16)
-    mixed = (
-        jnp.dot(normed, w_qkv, preferred_element_type=jnp.float32) + b_qkv.astype(jnp.float32)
-    ).astype(jnp.bfloat16)
-    shaped = mixed.reshape(block_total, BLOCK, 3, head_count, HEAD).astype(jnp.float32)
-    query_f = shaped[:, :, 0]
-    key_f = shaped[:, :, 1]
-    value_f = shaped[:, :, 2]
-    score_scale = 1.0 / math.sqrt(HEAD)
-    scores = jnp.einsum("bqhd,bkhd->bhqk", query_f, key_f) * score_scale
-    same_image = marks[:, :, None] == marks[:, None, :]
-    scores = jnp.where(same_image[:, None], scores, -1e30)
-    top_score = jnp.max(scores, axis=-1, keepdims=True)
-    expo = jnp.exp(scores - top_score)
-    probs_f = expo / jnp.sum(expo, axis=-1, keepdims=True)
-    probs_b = probs_f.astype(jnp.bfloat16)
-    attended = jnp.einsum("bhqk,bkhd->bqhd", probs_b.astype(jnp.float32), value_f)
-    attended = attended.reshape(block_total * BLOCK, inner).astype(jnp.bfloat16)
-    projected = jnp.dot(attended, w_out, preferred_element_type=jnp.float32) + b_out.astype(
-        jnp.float32
-    )
-    result = (rows + projected).astype(jnp.bfloat16)
-    return (result, (normed, query_f, key_f, value_f, probs_f, probs_b, attended))
-
-
-def output_backward(out_grad, saved, w_out):
-    normed, query_f, key_f, value_f, probs_f, probs_b, attended = saved
-    grad_out = jnp.dot(attended.T, out_grad, preferred_element_type=jnp.float32)
-    attn_grad = jnp.dot(out_grad, w_out.T, preferred_element_type=jnp.float32)
-    return (grad_out, attn_grad.reshape(query_f.shape))
-
-
-def qkv_backward(attn_grad, saved):
-    normed, query_f, key_f, value_f, probs_f, probs_b, attended = saved
-    score_scale = 1.0 / math.sqrt(HEAD)
-    prob_grad = jnp.einsum("bqhd,bkhd->bhqk", attn_grad, value_f)
-    value_grad = jnp.einsum("bhqk,bqhd->bkhd", probs_b.astype(jnp.float32), attn_grad)
-    score_grad = (
-        probs_f * (prob_grad - jnp.sum(prob_grad * probs_f, axis=-1, keepdims=True)) * score_scale
-    )
-    query_grad = jnp.einsum("bhqk,bkhd->bqhd", score_grad, key_f)
-    key_grad = jnp.einsum("bhqk,bqhd->bkhd", score_grad, query_f)
-    row_total = query_f.shape[0] * query_f.shape[1]
-    return [
-        jnp.dot(
-            normed.T,
-            part.reshape(row_total, -1).astype(jnp.bfloat16),
-            preferred_element_type=jnp.float32,
-        ).astype(jnp.bfloat16)
-        for part in (query_grad, key_grad, value_grad)
-    ]
 
 
 def local(
@@ -374,38 +461,16 @@
     balanced = cotangent.shape[0] // BLOCK
     width = patches.shape[1]
     devices = lax.axis_size("dp")
-    own_rank = lax.axis_index("dp")
-    segment, row_index, col_index, in_image = token_layout(patch_grids)
-    marks = jnp.stack([segment, row_index, col_index, in_image], axis=1).astype(jnp.float32)
-    marks = jnp.pad(marks, ((0, 0), (0, 8 - marks.shape[1]), (0, 0)))
+    images = patch_grids.shape[1]
+    marks = jnp.broadcast_to(
+        patch_grids.reshape(-1, 2 * images, 1).astype(jnp.float32),
+        (patch_grids.shape[0], 2 * images, BLOCK),
+    )
     rows, tags = balance(patches, marks, block_counts, send_counts, balanced)
-    live_count = block_counts[own_rank]
-    for section in range(send_counts.shape[0]):
-        sent_now = send_counts[section]
-        live_count = live_count - sent_now[own_rank] + sent_now[own_rank ^ (1 << section)]
-    rank_marks = tags[:, 0]
-    levels = jnp.arange(row_table.shape[0], dtype=jnp.float32)
-    here = tags[:, 3].reshape(-1, 1) > 0
-    row_hot = (here & (tags[:, 1].reshape(-1, 1) == levels)).astype(jnp.bfloat16)
-    col_hot = (here & (tags[:, 2].reshape(-1, 1) == levels)).astype(jnp.bfloat16)
-    table_sum = jnp.dot(row_hot, row_table, preferred_element_type=jnp.float32) + jnp.dot(
-        col_hot, col_table, preferred_element_type=jnp.float32
+    result, *parts = layer(
+        images, rows.reshape(balanced, BLOCK, width), tags, row_table, col_table,
+        ln_gain, ln_bias, w_qkv, b_qkv, w_out, b_out, cotangent,
     )
-    rank_blocks = (
-        (rows.reshape(-1, width).astype(jnp.float32) + table_sum)
-        .astype(jnp.bfloat16)
-        .reshape(balanced, BLOCK, width)
-    )
-    rank_live = jnp.arange(balanced, dtype=jnp.int32) < live_count
-    result, saved = layer_forward(
-        rank_blocks, rank_marks, ln_gain, ln_bias, w_qkv, b_qkv, w_out, b_out
-    )
-    slot_live = jnp.repeat(rank_live, BLOCK).reshape(-1, 1)
-    result = jnp.where(slot_live, result, jnp.zeros_like(result))
-    token_live = (rank_live[:, None] & (rank_marks >= 0)).reshape(-1, 1)
-    out_grad = jnp.where(token_live, cotangent, jnp.zeros_like(cotangent))
-    grad_out, attn_grad = output_backward(out_grad, saved, w_out)
-    parts = qkv_backward(attn_grad, saved) + [grad_out.astype(jnp.bfloat16)]
     qkv_rows, out_rows = reduce_rows(parts, devices)
     return (result, qkv_rows, out_rows)
 

time: 175 us -> 160 us (0.914)
  Pallas kernels: 98.5 us -> 141 us
  matrix products: 30.5 us -> 0 us
  local copies, waits for them, and re-layouts: 33.5 us -> 16.7 us
  between operations: 7.93 us -> 0.66 us
  other arithmetic: 3.96 us -> 0.69 us
    pallas_call x0 -> x1, Pallas kernels: none -> 42.6 us  [layer(): pl.pallas_call(functools.partial(layer_kernel, images), out_shape=(jax.Sh...]
    dot_general x14 -> x0, matrix products: 27.1 us -> none  [the longest x3 8.43 us: qkv_backward(): jnp.dot(normed.T, part.reshape(row_total, -1).astype(jnp.bfloat16), prefe...]
    slice x4 -> x0, local copies, waits for them, and re-layouts: 5.06 us -> none  [the longest x1 3.41 us: layer_forward(): query_f = shaped[:, :, 0]]
    unnamed x33 -> x12, local copies, waits for them, and re-layouts: 12.6 us -> 7.83 us
    reshape x2 -> x4, local copies, waits for them, and re-layouts: 8.77 us -> 5.13 us  [the longest x1 1.29 us: layer(): b_qkv.reshape(1, -1)]
    sub x1 -> x0, matrix products: 3.38 us -> none  [layer_forward(): expo = jnp.exp(scores - top_score)]
    dynamic_slice x4 -> x0, local copies, waits for them, and re-layouts: 3.25 us -> none  [the longest x3 1.89 us: local(): sent_now[own_rank ^ 1 << section]]
    reshape x1, local copies, waits for them, and re-layouts: 1.47 us -> 3.62 us  [reduce_rows(): part.reshape(devices // 2, 2, part.shape[0] // devices, part.shape[1])]
where the time goes in v2:
time: 160 us; the launch traced here: 159 us
  Pallas kernels  141 us (88%)
  local copies, waits for them, and re-layouts  16.7 us (10%)
    pallas_call x1, Pallas kernels, balance(): pl.pallas_call(functools.partial(balance_kernel, sections), out_shape=(ja...  50.5 us
    pallas_call x1, Pallas kernels, reduce_rows(): pl.pallas_call(functools.partial(reduce_kernel, orders), out_shape=(jax.S...  48.1 us
    pallas_call x1, Pallas kernels, layer(): pl.pallas_call(functools.partial(layer_kernel, images), out_shape=(jax.Sh...  42.6 us
    unnamed x12, local copies, waits for them, and re-layouts  7.83 us
    reshape x1, local copies, waits for them, and re-layouts, reduce_rows(): part.reshape(devices // 2, 2, part.shape[0] // devices, part.shape[1])  3.62 us

profile of v2, /device:TPU:0, one launch (start us, length us, event | category | flops | bytes accessed | tf_op | source)
XLA Modules:
  0.0 159.2 jit_solution(12520686618892606023)
XLA Ops:
  0.6 0.7 convert_element_type.11
  1.3 0.1 copy.17
  1.4 1.3 reshape.47.gain_ref
  2.7 1.3 reshape.48.bias_ref
  4.0 1.3 reshape.50.b_out_ref
  5.3 1.3 reshape.49.b_qkv_ref
  6.5 0.1 broadcast_in_dim.2.marks_ref
  6.6 0.0 copy-start
  6.6 1.5 copy-done
  8.2 0.0 copy-start.3
  8.2 0.7 copy-done.3
  8.8 0.0 copy-start.4
  8.8 0.7 copy-done.4
  9.5 50.5 %shard_map.148 = (bf16[4,8,16,1280]{3,2,1,0:T(8,128)(2,1)S(1)}, f32[4,16,128]{2,1,0:T(8,128)S(1)}) custom-call(s32[32]{0:T(128)S(1)} %copy-done.4, s32[5,32]{1,0:T(8,128)S(1)} %copy-done.3, bf16[6,8,16,1280]{3,2,1,0:T(8,128)(2,1)S(1)} %bitcast.6, f32[6,8,128]{2,1,0:T(8,128)S(1)} %broadcast_in_dim.2.marks_ref), custom_call_target="tpu_custom_call" | custom-call | tf_op jit(solution)/shard_map/pallas_call | solution.py:134
  60.0 0.0 copy-start.1
  60.0 1.1 copy-done.1
  61.1 0.0 copy-start.2
  61.1 0.6 copy-done.2
  61.7 42.6 %shard_map.149 = (bf16[512,1280]{1,0:T(8,128)(2,1)}, bf16[1280,640]{1,0:T(8,128)(2,1)}, bf16[1280,640]{1,0:T(8,128)(2,1)}, bf16[1280,640]{1,0:T(8,128)(2,1)}, bf16[640,1280]{1,0:T(8,128)(2,1)}) custom-call(bf16[4,128,1280]{2,1,0:T(8,128)(2,1)} %bitcast.7, f32[4,16,128]{2,1,0:T(8,128)} %copy-done.2, bf16[16,1280]{1,0:T(8,128)(2,1)} %row_ref.1, ...), custom_call_target="tpu_custom_call" | custom-call | tf_op jit(solution)/shard_map/pallas_call | solution.py:418
  104.3 3.6 %reshape.54.refs_3_ = bf16[16,2,20,1280]{3,2,1,0:T(8,128)(2,1)} reshape(bf16[640,1280]{1,0:T(8,128)(2,1)} %get-tuple-element.18) | data formatting | bytes 3276800 | tf_op jit(solution)/shard_map/reshape | solution.py:251
  107.9 48.1 %shard_map.150 = (f32[40,1920]{1,0:T(8,128)}, f32[20,1280]{1,0:T(8,128)}) custom-call(bf16[16,2,40,640]{3,2,1,0:T(8,128)(2,1)} %bitcast.8, bf16[16,2,40,640]{3,2,1,0:T(8,128)(2,1)} %bitcast.9, bf16[16,2,40,640]{3,2,1,0:T(8,128)(2,1)} %bitcast.10, bf16[16,2,20,1280]{3,2,1,0:T(8,128)(2,1)} %reshape.54.refs_3_), custom_call_target="tpu_custom_call" | custom-call | tf_op jit(solution)/shard_map/pallas_call | solution.py:262
  156.0 1.7 %copy.20 = f32[40,1920]{1,0:T(8,128)} copy(f32[40,1920]{1,0:T(8,128)} %get-tuple-element.25) | data formatting | bytes 614400
  157.7 1.6 copy.21
Async XLA Ops:
  6.6 1.5 copy-start
  8.2 0.7 copy-start.3
  8.8 0.7 copy-start.4
  60.0 1.1 copy-start.1
  61.1 0.6 copy-start.2

commit v3 on v2

--- a/solution.py
+++ b/solution.py
@@ -11,6 +11,10 @@
 HEAD = 80
 BLOCK = 128
 CHUNKS = 8
+GROUP = 8
+BALANCE_MIB = 20
+LAYER_MIB = 40
+REDUCE_MIB = 30
 EPSILON = 1e-06
 MESH = pl.DeviceIdType.MESH
 
@@ -152,15 +156,16 @@
             pltpu.SemaphoreType.DMA((sections,)),
         ],
         compiler_params=pltpu.CompilerParams(
-            collective_id=0, has_side_effects=True, vmem_limit_bytes=48 * 2**20
+            collective_id=0, has_side_effects=True, vmem_limit_bytes=BALANCE_MIB * 2**20
         ),
     )(block_counts, send_counts, patches.reshape(slot_count, CHUNKS, rows, width), marks)
 
 
-def reduce_kernel(orders, *refs):
+def reduce_kernel(orders, pieces, *refs):
     parts = len(orders)
     levels = len(orders[0])
-    ins, refs = refs[:parts], refs[parts:]
+    whole = pieces[-1][0] + 1
+    ins, refs = refs[:whole], refs[whole:]
     qkv_out, last_out = refs[0], refs[1]
     scratch = refs[2:]
     kept = [scratch[p * (levels + 1)] for p in range(parts)]
@@ -182,7 +187,7 @@
     def copy_of(p, s):
         bit = orders[p][s]
         if s == 0:
-            source = ins[p].at[:, 1 - side[0]]
+            source = ins[pieces[p][0]].at[:, 1 - side[0], :, pieces[p][1]]
         else:
             half = 1 << (levels - 1 - s)
             source = kept[p].at[
@@ -203,7 +208,7 @@
                 for i in range(1, levels):
                     chip = chip + ((j // (1 << (levels - 1 - i))) % 2) * (1 << (orders[p][i] - 1))
                 kept[p][j] = (
-                    ins[p][chip, side[0]].astype(jnp.float32) + land[p][0][chip].astype(jnp.float32)
+                    ins[pieces[p][0]][chip, side[0], :, pieces[p][1]].astype(jnp.float32) + land[p][0][chip].astype(jnp.float32)
                 ).astype(jnp.bfloat16)
                 return carry
 
@@ -221,11 +226,12 @@
             lax.fori_loop(0, total, step, 0)
             return
         final = kept[p][own].astype(jnp.float32) + land[p][s][0].astype(jnp.float32)
-        if p < parts - 1:
+        source, columns = pieces[p]
+        if source < whole - 1:
             width = final.shape[1]
-            qkv_out[:, p * width:(p + 1) * width] = final
+            qkv_out[:, source * width:(source + 1) * width] = final
         else:
-            last_out[...] = final
+            last_out[:, columns] = final
 
     for s in range(levels + 1):
         for p in range(parts):
@@ -239,37 +245,43 @@
             copy_of(p, s).wait_send()
 
 
-def reduce_rows(parts, devices):
+def reduce_rows(parts, last, devices):
     levels = devices.bit_length() - 1
     bits = list(range(1, levels))
+    shaped = [
+        part.reshape(devices // 2, 2, part.shape[0] // devices, part.shape[1]) for part in parts
+    ]
+    shaped.append(last.reshape(devices // 2, 2, last.shape[1], last.shape[2]))
+    count = len(shaped)
+    pieces = [(p, slice(0, part.shape[1])) for p, part in enumerate(parts)]
+    tiles = last.shape[2] // BLOCK
+    ends = [tiles * i // 3 * BLOCK for i in range(4)]
+    pieces += [(count - 1, slice(ends[i], ends[i + 1])) for i in range(3)]
     orders = []
-    for p in range(len(parts)):
+    for p in range(len(pieces)):
         first = bits[:3]
         turn = p % len(first)
         orders.append([0] + first[turn:] + first[:turn] + bits[3:])
-    shaped = [
-        part.reshape(devices // 2, 2, part.shape[0] // devices, part.shape[1]) for part in parts
-    ]
     vmem = pl.BlockSpec(memory_space=pltpu.VMEM)
     scratch = []
-    for part in shaped:
-        scratch.append(pltpu.VMEM((devices // 2,) + part.shape[2:], jnp.bfloat16))
+    for source, columns in pieces:
+        tile = (shaped[source].shape[2], columns.stop - columns.start)
+        scratch.append(pltpu.VMEM((devices // 2,) + tile, jnp.bfloat16))
         for s in range(levels):
-            scratch.append(pltpu.VMEM((1 << (levels - 1 - s),) + part.shape[2:], jnp.bfloat16))
-    count = len(parts)
-    scratch += [pltpu.SemaphoreType.DMA((count, levels))] * 2
-    qkv, last = shaped[0].shape, shaped[-1].shape
+            scratch.append(pltpu.VMEM((1 << (levels - 1 - s),) + tile, jnp.bfloat16))
+    scratch += [pltpu.SemaphoreType.DMA((len(pieces), levels))] * 2
+    qkv = shaped[0].shape
     return pl.pallas_call(
-        functools.partial(reduce_kernel, orders),
+        functools.partial(reduce_kernel, orders, pieces),
         out_shape=(
             jax.ShapeDtypeStruct((qkv[2], (count - 1) * qkv[3]), jnp.float32),
-            jax.ShapeDtypeStruct(last[2:], jnp.float32),
+            jax.ShapeDtypeStruct(last.shape[1:], jnp.float32),
         ),
         in_specs=[vmem] * count,
         out_specs=(vmem, vmem),
         scratch_shapes=scratch,
         compiler_params=pltpu.CompilerParams(
-            collective_id=1, has_side_effects=True, vmem_limit_bytes=56 * 2**20
+            collective_id=1, has_side_effects=True, vmem_limit_bytes=REDUCE_MIB * 2**20
         ),
     )(*shaped)
 
@@ -308,8 +320,7 @@
 
 
 def layer_kernel(
-    images, patches_ref, tags_ref, row_ref, col_ref, gain_ref, bias_ref, w_qkv_ref, b_qkv_ref,
-    w_out_ref, b_out_ref, cot_ref, out_ref, gq_ref, gk_ref, gv_ref, go_ref,
+    images, patches_ref, tags_ref, row_ref, col_ref, vector_ref, w_qkv_ref, w_out_ref, cot_ref, out_ref, gq_ref, gk_ref, gv_ref, go_ref,
     x_s, normed_s, grad_s, qkv_s, ag_s, att_s, dqkv_s, same_s,
 ):
     blocks = patches_ref.shape[0]
@@ -319,6 +330,9 @@
     levels = row_ref.shape[0]
     tables = jnp.concatenate([row_ref[...], col_ref[...]], axis=0)
     scale = 1.0 / math.sqrt(HEAD)
+    vectors = vector_ref[...].astype(jnp.float32)
+    gain, bias, b_out = (vectors[:, i * width:(i + 1) * width] for i in range(3))
+    b_qkv = vectors[:, 3 * width:]
 
     def embed(b, carry):
         rows = pl.ds(pl.multiple_of(b * BLOCK, BLOCK), BLOCK)
@@ -339,8 +353,8 @@
         centred = x - jnp.mean(x, axis=-1, keepdims=True)
         variance = jnp.mean(centred * centred, axis=-1, keepdims=True)
         normed_s[rows, :] = (
-            centred * lax.rsqrt(variance + EPSILON) * gain_ref[...].astype(jnp.float32)
-            + bias_ref[...].astype(jnp.float32)
+            centred * lax.rsqrt(variance + EPSILON) * gain
+            + bias
         ).astype(jnp.bfloat16)
         return carry
 
@@ -348,7 +362,7 @@
     for p in range(3):
         part = slice(p * inner, (p + 1) * inner)
         qkv_s[:, part] = (
-            dot(normed_s[...], w_qkv_ref[:, part]) + b_qkv_ref[:, part].astype(jnp.float32)
+            dot(normed_s[...], w_qkv_ref[:, part]) + b_qkv[:, part]
         ).astype(jnp.bfloat16)
     ag_s[...] = dot(grad_s[...], w_out_ref[...], COLS).astype(jnp.bfloat16)
 
@@ -358,22 +372,27 @@
         qkv = qkv_s[rows, :]
         outer = ag_s[rows, :]
         found = [[], [], [], []]
-        for h in range(heads):
-            part = [qkv[:, p * inner + h * HEAD:p * inner + (h + 1) * HEAD] for p in range(3)]
-            query, key, value = part
-            given = outer[:, h * HEAD:(h + 1) * HEAD]
-            scores = jnp.where(same, dot(query, key, COLS) * scale, -1e30)
-            expo = jnp.exp(scores - jnp.max(scores, axis=-1, keepdims=True))
-            probs = expo / jnp.sum(expo, axis=-1, keepdims=True)
-            probs_b = probs.astype(jnp.bfloat16)
-            found[3].append(dot(probs_b, value).astype(jnp.bfloat16))
-            prob_grad = dot(given, value, COLS)
-            score_grad = (
-                probs * (prob_grad - jnp.sum(prob_grad * probs, axis=-1, keepdims=True)) * scale
-            ).astype(jnp.bfloat16)
-            found[0].append(dot(score_grad, key).astype(jnp.bfloat16))
-            found[1].append(dot(score_grad, query, ROWS).astype(jnp.bfloat16))
-            found[2].append(dot(probs_b, given, ROWS).astype(jnp.bfloat16))
+        for first in range(0, heads, GROUP):
+            group = range(first, first + GROUP)
+            query, key, value = (
+                [qkv[:, p * inner + h * HEAD:p * inner + (h + 1) * HEAD] for h in group]
+                for p in range(3)
+            )
+            given = [outer[:, h * HEAD:(h + 1) * HEAD] for h in group]
+            scores = [dot(q, k, COLS) for q, k in zip(query, key)]
+            prob_grad = [dot(g, v, COLS) for g, v in zip(given, value)]
+            scores = [jnp.where(same, s * scale, -1e30) for s in scores]
+            expo = [jnp.exp(s - jnp.max(s, axis=-1, keepdims=True)) for s in scores]
+            probs = [e * (1.0 / jnp.sum(e, axis=-1, keepdims=True)) for e in expo]
+            probs_b = [p.astype(jnp.bfloat16) for p in probs]
+            score_grad = [
+                (p * (g - jnp.sum(g * p, axis=-1, keepdims=True)) * scale).astype(jnp.bfloat16)
+                for p, g in zip(probs, prob_grad)
+            ]
+            found[3] += [dot(p, v).astype(jnp.bfloat16) for p, v in zip(probs_b, value)]
+            found[2] += [dot(p, g, ROWS).astype(jnp.bfloat16) for p, g in zip(probs_b, given)]
+            found[0] += [dot(s, k).astype(jnp.bfloat16) for s, k in zip(score_grad, key)]
+            found[1] += [dot(s, q, ROWS).astype(jnp.bfloat16) for s, q in zip(score_grad, query)]
         for p in range(3):
             dqkv_s[rows, p * inner:(p + 1) * inner] = jnp.concatenate(found[p], axis=1)
         att_s[rows, :] = jnp.concatenate(found[3], axis=1)
@@ -384,7 +403,7 @@
     def project(b, carry):
         rows = pl.ds(pl.multiple_of(b * BLOCK, BLOCK), BLOCK)
         live = jnp.concatenate([tags_ref[b][8:9]] * (width // BLOCK), axis=1)
-        projected = dot(att_s[rows, :], w_out_ref[...]) + b_out_ref[...].astype(jnp.float32)
+        projected = dot(att_s[rows, :], w_out_ref[...]) + b_out
         total = x_s[rows, :].astype(jnp.float32) + projected
         out_ref[rows, :] = jnp.where(live > 0.5, total, 0.0).astype(jnp.bfloat16)
         return carry
@@ -402,15 +421,17 @@
 
     lax.fori_loop(0, width // tile, weigh, 0)
 
-    def weigh_out(i, carry):
-        rows = pl.ds(pl.multiple_of(i * BLOCK, BLOCK), BLOCK)
-        go_ref[rows, :] = dot(att_s[:, rows], grad_s[...], ROWS).astype(jnp.bfloat16)
-        return carry
-
-    lax.fori_loop(0, inner // BLOCK, weigh_out, 0)
-
-
-def layer(images, patches, tags, row_table, col_table, gain, bias, w_qkv, b_qkv, w_out, b_out, cot):
+    ranks, share = go_ref.shape[0], go_ref.shape[1]
+
+    for first in range(0, width, inner):
+        total = dot(att_s[...], grad_s[:, first:first + inner], ROWS)
+        for r in range(ranks):
+            go_ref[r, :, first:first + inner] = total[r * share:(r + 1) * share].astype(
+                jnp.bfloat16
+            )
+
+
+def layer(images, devices, patches, tags, row_table, col_table, gain, bias, w_qkv, b_qkv, w_out, b_out, cot):
     rows, width = cot.shape
     inner = w_out.shape[0]
     vmem = pl.BlockSpec(memory_space=pltpu.VMEM)
@@ -422,9 +443,9 @@
             jax.ShapeDtypeStruct((width, inner), half),
             jax.ShapeDtypeStruct((width, inner), half),
             jax.ShapeDtypeStruct((width, inner), half),
-            jax.ShapeDtypeStruct((inner, width), half),
+            jax.ShapeDtypeStruct((devices, inner // devices, width), half),
         ),
-        in_specs=[vmem] * 11,
+        in_specs=[vmem] * 8,
         out_specs=(vmem,) * 5,
         scratch_shapes=[
             pltpu.VMEM((rows, width), half),
@@ -436,10 +457,10 @@
             pltpu.VMEM((rows, 3 * inner), half),
             pltpu.VMEM((rows // BLOCK, BLOCK, BLOCK), jnp.float32),
         ],
-        compiler_params=pltpu.CompilerParams(vmem_limit_bytes=56 * 2**20),
+        compiler_params=pltpu.CompilerParams(vmem_limit_bytes=LAYER_MIB * 2**20),
     )(
-        patches, tags, row_table, col_table, gain.reshape(1, -1), bias.reshape(1, -1),
-        w_qkv, b_qkv.reshape(1, -1), w_out, b_out.reshape(1, -1), cot,
+        patches, tags, row_table, col_table,
+        jnp.concatenate([gain, bias, b_out, b_qkv]).reshape(1, -1), w_qkv, w_out, cot,
     )
 
 
@@ -468,10 +489,10 @@
     )
     rows, tags = balance(patches, marks, block_counts, send_counts, balanced)
     result, *parts = layer(
-        images, rows.reshape(balanced, BLOCK, width), tags, row_table, col_table,
+        images, devices, rows.reshape(balanced, BLOCK, width), tags, row_table, col_table,
         ln_gain, ln_bias, w_qkv, b_qkv, w_out, b_out, cotangent,
     )
-    qkv_rows, out_rows = reduce_rows(parts, devices)
+    qkv_rows, out_rows = reduce_rows(parts[:-1], parts[-1], devices)
     return (result, qkv_rows, out_rows)
 
 

time: 160 us -> 122 us (0.76)
  Pallas kernels: 141 us -> 114 us
  local copies, waits for them, and re-layouts: 16.7 us -> 5.75 us
    pallas_call x1, Pallas kernels: 42.6 us -> 22 us  [layer(): pl.pallas_call(functools.partial(layer_kernel, images), out_shape=(jax.Sh...]
    reshape x5 -> x1, local copies, waits for them, and re-layouts: 8.75 us -> 0.02 us  [layer(): jnp.concatenate([gain, bias, b_out, b_qkv]).reshape(1, -1)]
    pallas_call x1, Pallas kernels: 48.1 us -> 41.7 us  [reduce_rows(): pl.pallas_call(functools.partial(reduce_kernel, orders, pieces), out_shap...]
    unnamed x12 -> x16, local copies, waits for them, and re-layouts: 7.83 us -> 5.58 us
where the time goes in v3:
time: 122 us
  Pallas kernels  114 us (93%)
  local copies, waits for them, and re-layouts  5.75 us (5%)
  other arithmetic  1.46 us (1%)
    pallas_call x1, Pallas kernels, balance(): pl.pallas_call(functools.partial(balance_kernel, sections), out_shape=(ja...  50.5 us
    pallas_call x1, Pallas kernels, reduce_rows(): pl.pallas_call(functools.partial(reduce_kernel, orders, pieces), out_shap...  41.7 us
    pallas_call x1, Pallas kernels, layer(): pl.pallas_call(functools.partial(layer_kernel, images), out_shape=(jax.Sh...  22 us
    unnamed x16, local copies, waits for them, and re-layouts  5.58 us

profile of v3, /device:TPU:0, one launch (start us, length us, event | category | flops | bytes accessed | tf_op | source)
XLA Modules:
  0.0 122.1 jit_solution(16090797917923467479)
XLA Ops:
  0.6 0.0 copy-start.4
  0.6 0.0 copy-start.3
  0.7 0.7 convert_element_type.11
  1.4 0.1 copy.16
  1.4 0.7 pad_maximum_fusion
  2.2 0.1 broadcast_in_dim.2.marks_ref
  2.3 0.0 copy-start
  2.3 1.5 %copy-done = bf16[768,1280]{1,0:T(8,128)(2,1)S(1)} copy-done((bf16[768,1280]{1,0:T(8,128)(2,1)S(1)}, bf16[768,1280]{1,0:T(8,128)(2,1)}, u32[]{:S(2)}) %copy-start) | copy-done | bytes 1966104
  3.8 0.0 copy-start.5
  3.8 0.7 copy-done.5
  4.5 0.0 copy-start.6
  4.5 0.7 copy-done.6
  5.2 0.0 copy-start.1
  5.2 50.5 %shard_map.148 = (bf16[4,8,16,1280]{3,2,1,0:T(8,128)(2,1)S(1)}, f32[4,16,128]{2,1,0:T(8,128)S(1)}) custom-call(s32[32]{0:T(128)S(1)} %copy-done.6, s32[5,32]{1,0:T(8,128)S(1)} %copy-done.5, bf16[6,8,16,1280]{3,2,1,0:T(8,128)(2,1)S(1)} %bitcast.7, f32[6,8,128]{2,1,0:T(8,128)S(1)} %broadcast_in_dim.2.marks_ref), custom_call_target="tpu_custom_call" | custom-call | tf_op jit(solution)/shard_map/pallas_call | solution.py:138
  55.7 0.0 copy-done.4
  55.7 0.0 copy-done.3
  55.7 0.0 copy-done.1
  55.7 0.0 copy-start.2
  55.7 1.3 %copy-done.2 = bf16[512,1280]{1,0:T(8,128)(2,1)S(1)} copy-done((bf16[512,1280]{1,0:T(8,128)(2,1)S(1)}, bf16[512,1280]{1,0:T(8,128)(2,1)}, u32[]{:S(2)}) %copy-start.2) | copy-done | bytes 1310744
  57.0 22.0 %shard_map.149 = (bf16[512,1280]{1,0:T(8,128)(2,1)}, bf16[1280,640]{1,0:T(8,128)(2,1)S(1)}, bf16[1280,640]{1,0:T(8,128)(2,1)S(1)}, bf16[1280,640]{1,0:T(8,128)(2,1)S(1)}, bf16[32,20,1280]{2,1,0:T(8,128)(2,1)S(1)}) custom-call(bf16[4,128,1280]{2,1,0:T(8,128)(2,1)S(1)} %bitcast.12, f32[4,16,128]{2,1,0:T(8,128)S(1)} %get-tuple-element.13.tags_ref, ...), custom_call_target="tpu_custom_call" | custom-call | tf_op jit(solution)/shard_map/pallas_call | solution.py:439
  79.0 41.7 %shard_map.150 = (f32[40,1920]{1,0:T(8,128)S(1)}, f32[20,1280]{1,0:T(8,128)S(1)}) custom-call(bf16[16,2,40,640]{3,2,1,0:T(8,128)(2,1)S(1)} %bitcast.9, bf16[16,2,40,640]{3,2,1,0:T(8,128)(2,1)S(1)} %bitcast.10, bf16[16,2,40,640]{3,2,1,0:T(8,128)(2,1)S(1)} %bitcast.11, bf16[16,2,20,1280]{3,2,1,0:T(8,128)(2,1)S(1)} %bitcast.8), custom_call_target="tpu_custom_call" | custom-call | tf_op jit(solution)/shard_map/pallas_call | solution.py:274
  120.7 0.7 copy.19
  121.5 0.6 copy.20
  (1 shorter events, 0.0 us)
Async XLA Ops:
  0.6 55.0 %copy-start.4 = (bf16[16,1280]{1,0:T(8,128)(2,1)S(1)}, bf16[16,1280]{1,0:T(8,128)(2,1)}, u32[]{:S(2)}) copy-start(bf16[16,1280]{1,0:T(8,128)(2,1)} %col_ref.1) | copy-start | bytes 122884
  0.6 55.0 %copy-start.3 = (bf16[16,1280]{1,0:T(8,128)(2,1)S(1)}, bf16[16,1280]{1,0:T(8,128)(2,1)}, u32[]{:S(2)}) copy-start(bf16[16,1280]{1,0:T(8,128)(2,1)} %row_ref.1) | copy-start | bytes 122884
  2.3 1.5 %copy-start = (bf16[768,1280]{1,0:T(8,128)(2,1)S(1)}, bf16[768,1280]{1,0:T(8,128)(2,1)}, u32[]{:S(2)}) copy-start(bf16[768,1280]{1,0:T(8,128)(2,1)} %param.13) | copy-start | bytes 5898244
  3.8 0.7 copy-start.5
  4.5 0.7 copy-start.6
  5.2 50.5 %copy-start.1 = (bf16[640,1280]{1,0:T(8,128)(2,1)S(1)}, bf16[640,1280]{1,0:T(8,128)(2,1)}, u32[]{:S(2)}) copy-start(bf16[640,1280]{1,0:T(8,128)(2,1)} %w_out_ref.1) | copy-start | bytes 4915204
  55.7 1.3 %copy-start.2 = (bf16[512,1280]{1,0:T(8,128)(2,1)S(1)}, bf16[512,1280]{1,0:T(8,128)(2,1)}, u32[]{:S(2)}) copy-start(bf16[512,1280]{1,0:T(8,128)(2,1)} %cot_ref.1) | copy-start | bytes 3932164

commit v4 on v3

--- a/solution.py
+++ b/solution.py
@@ -164,7 +164,7 @@
 def reduce_kernel(orders, pieces, *refs):
     parts = len(orders)
     levels = len(orders[0])
-    whole = pieces[-1][0] + 1
+    whole = max(source for source, _ in pieces) + 1
     ins, refs = refs[:whole], refs[whole:]
     qkv_out, last_out = refs[0], refs[1]
     scratch = refs[2:]
@@ -257,6 +257,7 @@
     tiles = last.shape[2] // BLOCK
     ends = [tiles * i // 3 * BLOCK for i in range(4)]
     pieces += [(count - 1, slice(ends[i], ends[i + 1])) for i in range(3)]
+    pieces = pieces[3:] + pieces[:3]
     orders = []
     for p in range(len(pieces)):
         first = bits[:3]

time: 122 us -> 119 us (0.975)
  Pallas kernels: 114 us -> 110 us
    pallas_call x1, Pallas kernels: 41.7 us -> 38 us  [reduce_rows(): pl.pallas_call(functools.partial(reduce_kernel, orders, pieces), out_shap...]
where the time goes in v4:
time: 119 us; the launch traced here: 118 us
  Pallas kernels  110 us (92%)
  local copies, waits for them, and re-layouts  5.75 us (5%)
  other arithmetic  1.46 us (1%)
    pallas_call x1, Pallas kernels, balance(): pl.pallas_call(functools.partial(balance_kernel, sections), out_shape=(ja...  50.5 us
    pallas_call x1, Pallas kernels, reduce_rows(): pl.pallas_call(functools.partial(reduce_kernel, orders, pieces), out_shap...  38 us
    pallas_call x1, Pallas kernels, layer(): pl.pallas_call(functools.partial(layer_kernel, images), out_shape=(jax.Sh...  22 us
    unnamed x16, local copies, waits for them, and re-layouts  5.58 us

profile of v4, /device:TPU:0, one launch (start us, length us, event | category | flops | bytes accessed | tf_op | source)
XLA Modules:
  0.0 118.4 jit_solution(18385468221445152755)
XLA Ops:
  0.6 0.0 copy-start.4
  0.6 0.0 copy-start.3
  0.7 0.7 convert_element_type.11
  1.4 0.1 copy.16
  1.4 0.7 pad_maximum_fusion
  2.2 0.1 broadcast_in_dim.2.marks_ref
  2.3 0.0 copy-start
  2.3 1.5 %copy-done = bf16[768,1280]{1,0:T(8,128)(2,1)S(1)} copy-done((bf16[768,1280]{1,0:T(8,128)(2,1)S(1)}, bf16[768,1280]{1,0:T(8,128)(2,1)}, u32[]{:S(2)}) %copy-start) | copy-done | bytes 1966104
  3.8 0.0 copy-start.5
  3.8 0.7 copy-done.5
  4.5 0.0 copy-start.6
  4.5 0.7 copy-done.6
  5.2 0.0 copy-start.1
  5.2 50.5 %shard_map.148 = (bf16[4,8,16,1280]{3,2,1,0:T(8,128)(2,1)S(1)}, f32[4,16,128]{2,1,0:T(8,128)S(1)}) custom-call(s32[32]{0:T(128)S(1)} %copy-done.6, s32[5,32]{1,0:T(8,128)S(1)} %copy-done.5, bf16[6,8,16,1280]{3,2,1,0:T(8,128)(2,1)S(1)} %bitcast.7, f32[6,8,128]{2,1,0:T(8,128)S(1)} %broadcast_in_dim.2.marks_ref), custom_call_target="tpu_custom_call" | custom-call | tf_op jit(solution)/shard_map/pallas_call | solution.py:138
  55.7 0.0 copy-done.4
  55.7 0.0 copy-done.3
  55.7 0.0 copy-done.1
  55.7 0.0 copy-start.2
  55.7 1.3 %copy-done.2 = bf16[512,1280]{1,0:T(8,128)(2,1)S(1)} copy-done((bf16[512,1280]{1,0:T(8,128)(2,1)S(1)}, bf16[512,1280]{1,0:T(8,128)(2,1)}, u32[]{:S(2)}) %copy-start.2) | copy-done | bytes 1310744
  57.0 22.0 %shard_map.149 = (bf16[512,1280]{1,0:T(8,128)(2,1)}, bf16[1280,640]{1,0:T(8,128)(2,1)S(1)}, bf16[1280,640]{1,0:T(8,128)(2,1)S(1)}, bf16[1280,640]{1,0:T(8,128)(2,1)S(1)}, bf16[32,20,1280]{2,1,0:T(8,128)(2,1)S(1)}) custom-call(bf16[4,128,1280]{2,1,0:T(8,128)(2,1)S(1)} %bitcast.12, f32[4,16,128]{2,1,0:T(8,128)S(1)} %get-tuple-element.13.tags_ref, ...), custom_call_target="tpu_custom_call" | custom-call | tf_op jit(solution)/shard_map/pallas_call | solution.py:440
  79.0 38.0 %shard_map.150 = (f32[40,1920]{1,0:T(8,128)S(1)}, f32[20,1280]{1,0:T(8,128)S(1)}) custom-call(bf16[16,2,40,640]{3,2,1,0:T(8,128)(2,1)S(1)} %bitcast.9, bf16[16,2,40,640]{3,2,1,0:T(8,128)(2,1)S(1)} %bitcast.10, bf16[16,2,40,640]{3,2,1,0:T(8,128)(2,1)S(1)} %bitcast.11, bf16[16,2,20,1280]{3,2,1,0:T(8,128)(2,1)S(1)} %bitcast.8), custom_call_target="tpu_custom_call" | custom-call | tf_op jit(solution)/shard_map/pallas_call | solution.py:275
  117.0 0.7 copy.19
  117.8 0.6 copy.20
  (1 shorter events, 0.0 us)
Async XLA Ops:
  0.6 55.0 %copy-start.4 = (bf16[16,1280]{1,0:T(8,128)(2,1)S(1)}, bf16[16,1280]{1,0:T(8,128)(2,1)}, u32[]{:S(2)}) copy-start(bf16[16,1280]{1,0:T(8,128)(2,1)} %col_ref.1) | copy-start | bytes 122884
  0.6 55.0 %copy-start.3 = (bf16[16,1280]{1,0:T(8,128)(2,1)S(1)}, bf16[16,1280]{1,0:T(8,128)(2,1)}, u32[]{:S(2)}) copy-start(bf16[16,1280]{1,0:T(8,128)(2,1)} %row_ref.1) | copy-start | bytes 122884
  2.3 1.5 %copy-start = (bf16[768,1280]{1,0:T(8,128)(2,1)S(1)}, bf16[768,1280]{1,0:T(8,128)(2,1)}, u32[]{:S(2)}) copy-start(bf16[768,1280]{1,0:T(8,128)(2,1)} %param.13) | copy-start | bytes 5898244
  3.8 0.7 copy-start.5
  4.5 0.7 copy-start.6
  5.2 50.5 %copy-start.1 = (bf16[640,1280]{1,0:T(8,128)(2,1)S(1)}, bf16[640,1280]{1,0:T(8,128)(2,1)}, u32[]{:S(2)}) copy-start(bf16[640,1280]{1,0:T(8,128)(2,1)} %w_out_ref.1) | copy-start | bytes 4915204
  55.7 1.3 %copy-start.2 = (bf16[512,1280]{1,0:T(8,128)(2,1)S(1)}, bf16[512,1280]{1,0:T(8,128)(2,1)}, u32[]{:S(2)}) copy-start(bf16[512,1280]{1,0:T(8,128)(2,1)} %cot_ref.1) | copy-start | bytes 3932164
